TPU v7x, 256 devices: a whole 4x4x8 slice. The times are simulated.
256 devices in a mesh: boxgrp: 64 (over z, y, core), sub: 4 (over x).
Axes of the slice: x: 4, y: 4, z: 8, core: 2. Of those that a mesh axis runs over, the one named last changes fastest.
Arguments:
- coarse_velocity: float32 [3, 1024, 64, 32], P(None, ('boxgrp', 'sub')), may hold values from -6 to 6
- coarse_pressure: float32 [1024, 64, 32], P(('boxgrp', 'sub')), may hold values from -6 to 6
- coarse_viscosity: float32 [1024, 64, 32], P(('boxgrp', 'sub')), may hold values from 0.1 to 10
- coarse_force: float32 [3, 1024, 64, 32], P(None, ('boxgrp', 'sub')), may hold values from -6 to 6
- refined_velocity_field: float32 [3, 32, 64, 64, 64], P(None, 'sub', 'boxgrp'), may hold values from -6 to 6
- refined_pressure_field: float32 [32, 64, 64, 64], P('sub', 'boxgrp'), may hold values from -6 to 6
- refined_viscosity_field: float32 [32, 64, 64, 64], P('sub', 'boxgrp'), may hold values from 0.1 to 10
- refined_body_force: float32 [3, 32, 64, 64, 64], P(None, 'sub', 'boxgrp'), may hold values from -6 to 6
- box_spots: int32 [64], replicated, may hold values from -1 to 1, as said below
Outputs:
- new_coarse_velocity: float32 [3, 1024, 64, 32], P(None, ('boxgrp', 'sub'))
- new_coarse_pressure: float32 [1024, 64, 32], P(('boxgrp', 'sub'))
- new_fine_velocity: float32 [3, 32, 64, 64, 64], P(None, 'sub', 'boxgrp')
- new_fine_pressure: float32 [32, 64, 64, 64], P('sub', 'boxgrp')
Inputs may be any that keep to these rules, and one draw needn't show every extreme that they name: `box_spots`: slot j belongs to group j and holds the place q (0 or 1) of its fine box along y in that group's slab, or -1 if the slot is empty. The places of one group differ, two consecutive groups share no place, and some group fills all 1 slots.
All inputs are finite; a program needn't handle non-finite values.
Results may differ from a plain program's by a relative error of at most 0.0003.
Values sent between devices are 32-bit elements; how exact they have to be, the bound alone decides.
A program may use at most 64 MiB of HBM per device.

v0:
```python
from functools import partial
from functools import reduce

import jax
import jax.numpy as jnp
from jax import lax
from jax.sharding import PartitionSpec as P

SWEEPS = 2


RELAX_SCALE = 1.25
DAMPING = 0.8
PRECISE = lax.Precision.HIGHEST


def padded_2(shard, sides, width):
    edges = {}
    for axis, dim in sides:
        devices, length = (lax.axis_size(axis), shard.shape[dim])
        up = [(i, (i + 1) % devices) for i in range(devices - 1)]
        last = lax.slice_in_dim(shard, length - width, length, axis=dim)
        leading = lax.slice_in_dim(shard, 0, width, axis=dim)
        edges[dim] = (
            lax.ppermute(last, axis, up),
            lax.ppermute(leading, axis, [(b, a) for a, b in up]),
        )
    done = []
    for _, dim in sides:
        low, high = edges[dim]
        around = [(width, width) if d in done else (0, 0) for d in range(shard.ndim)]
        shard = jnp.concatenate([jnp.pad(low, around), shard, jnp.pad(high, around)], axis=dim)
        done.append(dim)
    return shard


def with_halo(block, sides, width):
    for axis, dim in sides:
        count = lax.axis_size(axis)
        forward = [(i, i + 1) for i in range(count - 1)]
        backward = [(target, source) for source, target in forward]
        low = lax.ppermute(
            lax.slice_in_dim(block, block.shape[dim] - width, None, axis=dim), axis, forward
        )
        high = lax.ppermute(lax.slice_in_dim(block, 0, width, axis=dim), axis, backward)
        block = jnp.concatenate([low, block, high], axis=dim)
    return block


def add_all(terms):
    return reduce(lambda left_v, right_v: left_v + right_v, terms)


def center(field_in, planes):
    start_at = (field_in.shape[1] - planes) // 2
    return lax.slice_in_dim(field_in, start_at, start_at + planes, axis=1)


def beside_all(padded):
    middle = padded[:, 1:-1, :, 1:-1, 1:-1]
    beside = [
        padded[:, :-2, :, 1:-1, 1:-1],
        padded[:, 2:, :, 1:-1, 1:-1],
        padded[:, 1:-1, :, :-2, 1:-1],
        padded[:, 1:-1, :, 2:, 1:-1],
        padded[:, 1:-1, :, 1:-1, :-2],
        padded[:, 1:-1, :, 1:-1, 2:],
    ]
    return (middle, beside)


def divergence(beside, inv_two):
    return (
        beside[1][0:1]
        - beside[0][0:1]
        + (beside[3][1:2] - beside[2][1:2])
        + (beside[5][2:3] - beside[4][2:3])
    ) * inv_two


def gradient(beside, inv_two):
    return (
        jnp.concatenate([beside[1] - beside[0], beside[3] - beside[2], beside[5] - beside[4]], 0)
        * inv_two
    )


def first_section(padded, force, inv_sq, inv_two):
    mu_mid, mu_beside = beside_all(padded[4:5])
    mu_faces = [0.5 * (mu_mid + nearby) for nearby in mu_beside]
    diag_a = inv_sq * add_all(mu_faces)
    vel_mid, vel_beside = beside_all(padded[0:3])
    apply_a = inv_sq * add_all(
        [mu_face * (vel_mid - nearby) for mu_face, nearby in zip(mu_faces, vel_beside)]
    )
    pres_mid, pres_beside = beside_all(padded[3:4])
    resid_u = force - apply_a - gradient(pres_beside, inv_two)
    resid_p = -divergence(vel_beside, inv_two)
    relaxed = resid_u / (RELAX_SCALE * diag_a)
    return (relaxed, diag_a, resid_p)


def second_section(padded, resid_p, inv_sq, inv_two):
    rel_mid, rel_beside = beside_all(padded[0:3])
    source = resid_p - divergence(rel_beside, inv_two)
    diag_mid, diag_beside = beside_all(padded[3:4])
    weights = [2.0 / (RELAX_SCALE * (diag_mid + nearby)) for nearby in diag_beside]
    diag_s = inv_sq * add_all(weights)
    return (source, weights, diag_s, DAMPING * source / diag_s)


def jacobi_sweep(padded, source, weights, diag_s, inv_sq):
    upd_mid, upd_beside = beside_all(padded)
    apply_s = inv_sq * add_all(
        [weight * (upd_mid - nearby) for weight, nearby in zip(weights, upd_beside)]
    )
    return upd_mid + DAMPING * (source - apply_s) / diag_s


def last_section(padded, relaxed, diag_a, velocity, pressure, inv_two):
    upd_mid, upd_beside = beside_all(padded)
    return (
        velocity + relaxed - gradient(upd_beside, inv_two) / (RELAX_SCALE * diag_a),
        pressure + upd_mid,
    )


def run_level(state, force, pad_state, pad_corr, refresh, fixing, inv_sq, inv_two):
    relaxed, diag_a, resid_p = first_section(pad_state(state), force, inv_sq, inv_two)
    relaxed = fixing(relaxed)
    diag_a = fixing(diag_a)
    stacked = pad_corr(refresh(jnp.concatenate([relaxed, diag_a], 0)))
    planes = stacked.shape[1] - 2
    source, weights, diag_s, update = second_section(
        stacked, center(resid_p, planes), inv_sq, inv_two
    )
    update = fixing(update)
    padded = pad_corr(refresh(update))
    planes = padded.shape[1] - 2
    update = fixing(
        jacobi_sweep(
            padded,
            center(source, planes),
            [center(weight, planes) for weight in weights],
            center(diag_s, planes),
            inv_sq,
        )
    )
    padded = pad_corr(refresh(update))
    planes = padded.shape[1] - 2
    return last_section(
        padded,
        center(relaxed, planes),
        center(diag_a, planes),
        center(state[0:3], planes),
        center(state[3:4], planes),
        inv_two,
    )


def pad_flat(field_in):
    return jnp.pad(field_in, ((0, 0), (0, 0), (0, 0), (1, 1), (1, 1)))


def keep_same(field_in):
    return field_in


def link_tables(slot_spots, group_of, columns):
    spot_row = slot_spots[:, None]
    spot_col = slot_spots[None, :]
    usable = (spot_row >= 0) & (spot_col >= 0) & (group_of[:, None] == group_of[None, :])
    row_place = spot_row // columns
    col_place = spot_row % columns
    matches = [
        usable & (spot_col == spot_row - columns) & (row_place > 0),
        usable & (spot_col == spot_row + columns),
        usable & (spot_col == spot_row - 1) & (col_place > 0),
        usable & (spot_col == spot_row + 1) & (col_place < columns - 1),
    ]
    tables = [matrix.astype(jnp.float32) for matrix in matches]
    return (tables, [jnp.sum(matrix, axis=1) for matrix in tables])


def fetch_row(matrix, edge_rows):
    return jnp.einsum("jm,kwmx->kwjx", matrix, edge_rows, precision=PRECISE)


def side_pad(field_in, border, links):
    tables, counts_nb = links
    if border is None:
        border = jnp.zeros(
            field_in.shape[:3] + (field_in.shape[3] + 2, field_in.shape[4] + 2), field_in.dtype
        )
    row_low = jnp.where(
        counts_nb[0][:, None] > 0,
        fetch_row(tables[0], field_in[:, :, :, -1, :]),
        border[:, :, :, 0, 1:-1],
    )
    row_high = jnp.where(
        counts_nb[1][:, None] > 0,
        fetch_row(tables[1], field_in[:, :, :, 0, :]),
        border[:, :, :, -1, 1:-1],
    )
    middle = jnp.concatenate([row_low[:, :, :, None], field_in, row_high[:, :, :, None]], 3)
    col_low = jnp.where(
        counts_nb[2][:, None] > 0,
        fetch_row(tables[2], field_in[:, :, :, :, -1]),
        border[:, :, :, 1:-1, 0],
    )
    col_high = jnp.where(
        counts_nb[3][:, None] > 0,
        fetch_row(tables[3], field_in[:, :, :, :, 0]),
        border[:, :, :, 1:-1, -1],
    )
    col_low = jnp.concatenate([border[:, :, :, 0:1, 0], col_low, border[:, :, :, -1:, 0]], 3)
    col_high = jnp.concatenate([border[:, :, :, 0:1, -1], col_high, border[:, :, :, -1:, -1]], 3)
    return jnp.concatenate([col_low[..., None], middle, col_high[..., None]], 4)


def upsample(coarse_block):
    return jnp.repeat(jnp.repeat(jnp.repeat(coarse_block, 2, axis=1), 2, axis=2), 2, axis=3)


def coarsen(field_in):
    shaped = field_in.reshape(
        field_in.shape[0],
        field_in.shape[1] // 2,
        2,
        field_in.shape[2],
        field_in.shape[3] // 2,
        2,
        field_in.shape[4] // 2,
        2,
    )
    return 0.125 * jnp.sum(shaped, axis=(2, 5, 7))


def plane_valid(planes, base, limit, inner):
    extra = (planes - inner) // 2
    index_all = base + jnp.arange(planes, dtype=jnp.int32) - extra
    return ((index_all >= 0) & (index_all < limit))[None, :, None, None, None]


def fix_planes(field_in, base, limit, inner):
    return jnp.where(plane_valid(field_in.shape[1], base, limit, inner), field_in, 0.0)


def on_device(
    coarse_velocity,
    coarse_pressure,
    coarse_viscosity,
    coarse_force,
    refined_velocity_field,
    refined_pressure_field,
    refined_viscosity_field,
    refined_body_force,
    box_spots,
):
    sub_size = lax.axis_size("sub")
    group_no = lax.axis_index("boxgrp")
    sub_no = lax.axis_index("sub")
    device_no = group_no * sub_size + sub_no
    coarse_planes = coarse_velocity.shape[1]
    fine_planes = refined_velocity_field.shape[1]
    slot_total = refined_velocity_field.shape[2]
    half_y = refined_velocity_field.shape[3] // 2
    half_x = refined_velocity_field.shape[4] // 2
    spot_rows = coarse_velocity.shape[2] // half_y
    spot_cols = coarse_velocity.shape[3] // half_x
    slot_spots = lax.dynamic_slice_in_dim(box_spots, group_no * slot_total, slot_total)
    links = link_tables(slot_spots, jnp.zeros_like(slot_spots), spot_cols)
    coarse_state = jnp.concatenate(
        [coarse_velocity, coarse_pressure[None], coarse_viscosity[None]], 0
    )[:, :, None]
    fine_state = jnp.concatenate(
        [refined_velocity_field, refined_pressure_field[None], refined_viscosity_field[None]], 0
    )
    ghost_depth = SWEEPS + 2
    coarse_ext = padded_2(
        jnp.concatenate([coarse_state, coarse_force[:, :, None]], 0),
        ((("boxgrp", "sub"), 1),),
        SWEEPS + 2,
    )
    fine_ext = with_halo(
        jnp.concatenate([fine_state, refined_body_force], 0), (("sub", 1),), SWEEPS + 2
    )
    coarse_push = center(coarse_ext[5:8], coarse_planes + 2 * ghost_depth - 2)
    fine_push = center(fine_ext[5:8], fine_planes + 2 * ghost_depth - 2)
    coarse_ext = coarse_ext[0:5]
    fine_ext = fine_ext[0:5]
    all_planes = coarse_planes * lax.axis_size("boxgrp") * sub_size
    coarse_fix = partial(
        fix_planes, base=device_no * coarse_planes, limit=all_planes, inner=coarse_planes
    )
    fine_fix = partial(
        fix_planes, base=sub_no * fine_planes, limit=fine_planes * sub_size, inner=fine_planes
    )
    coarse_vel_new, coarse_pres_new = run_level(
        coarse_ext, coarse_push, pad_flat, pad_flat, keep_same, coarse_fix, 1.0, 0.5
    )
    state_planes = fine_ext.shape[1]
    coarse_pad = jnp.pad(coarse_ext[:, :, 0], ((0, 0), (0, 0), (1, 1), (1, 1)))

    def inject_one(spot_no):
        spot_safe = jnp.maximum(spot_no, 0)
        start_y = spot_safe // spot_cols * half_y
        start_x = spot_safe % spot_cols * half_x
        coarse_block = lax.dynamic_slice(
            coarse_pad,
            (jnp.int32(0), jnp.int32(0), start_y, start_x),
            (5, coarse_pad.shape[1], half_y + 2, half_x + 2),
        )
        raised = upsample(coarse_block)
        return lax.slice_in_dim(raised, ghost_depth, ghost_depth + state_planes, axis=1)[
            :, :, 1:-1, 1:-1
        ]

    injection = jax.vmap(inject_one)(slot_spots).transpose(1, 2, 0, 3, 4)
    valid_fine = plane_valid(
        state_planes, sub_no * fine_planes, fine_planes * sub_size, fine_planes
    )
    fine_ext = jnp.where(valid_fine, fine_ext, injection[:, :, :, 1:-1, 1:-1])
    fine_vel_new, fine_pres_new = run_level(
        fine_ext,
        fine_push,
        partial(side_pad, border=injection, links=links),
        partial(side_pad, border=None, links=links),
        keep_same,
        fine_fix,
        4.0,
        1.0,
    )
    occupied = (slot_spots >= 0).astype(jnp.float32)[None, None, :, None, None]
    fine_vel_new = fine_vel_new * occupied
    fine_pres_new = fine_pres_new * occupied
    onehot = (
        slot_spots[:, None] == jnp.arange(spot_rows * spot_cols, dtype=jnp.int32)[None, :]
    ).astype(jnp.float32)
    onehot = onehot.reshape(slot_total, spot_rows, spot_cols)
    averaged = coarsen(jnp.concatenate([fine_vel_new, fine_pres_new], 0))
    placed = jnp.einsum("kzjyx,jab->kzaybx", averaged, onehot, precision=PRECISE)
    placed = placed.reshape(4, coarse_planes, coarse_velocity.shape[2], coarse_velocity.shape[3])
    covered = jnp.repeat(jnp.repeat(jnp.sum(onehot, 0), half_y, 0), half_x, 1)
    coarse_all = jnp.concatenate([coarse_vel_new, coarse_pres_new], 0)[:, :, 0]
    coarse_all = jnp.where(covered[None, None] > 0, placed, coarse_all)
    return (coarse_all[0:3], coarse_all[3], fine_vel_new, fine_pres_new[0])


def solution(mesh):
    return jax.shard_map(
        on_device,
        mesh=mesh,
        in_specs=(
            P(None, ("boxgrp", "sub"), None, None),
            P(("boxgrp", "sub"), None, None),
            P(("boxgrp", "sub"), None, None),
            P(None, ("boxgrp", "sub"), None, None),
            P(None, "sub", "boxgrp", None, None),
            P("sub", "boxgrp", None, None),
            P("sub", "boxgrp", None, None),
            P(None, "sub", "boxgrp", None, None),
            P(),
        ),
        out_specs=(
            P(None, ("boxgrp", "sub"), None, None),
            P(("boxgrp", "sub"), None, None),
            P(None, "sub", "boxgrp", None, None),
            P("sub", "boxgrp", None, None),
        ),
        check_vma=False,
    )
```

profile of v0, /device:TPU:130, one launch (start us, length us, event | category | flops | bytes accessed | tf_op | source)
XLA Modules:
  0.0 111.1 jit_solution(13768193525297489433)
XLA Ops:
  0.7 1.1 %maximum_bitcast_fusion = f32[5,4,1,64,32]{3,4,1,0,2:T(8,128)S(1)} fusion(f32[1,4,64,32]{2,3,1,0:T(8,128)} %bitcast.108, f32[1,4,64,32]{2,3,1,0:T(8,128)} %bitcast.107, f32[3,4,64,32]{2,3,1,0:T(8,128)} %param.9), kind=kLoop, calls=%fused_computation.213 | loop fusion | flops 81920 | bytes 327680 | tf_op jit(solution)/shard_map/broadcast_in_dim | solution.py:273
  1.8 1.0 pad_maximum_fusion.34
  2.8 3.4 %collective-permute-start.2 = (f32[8,4,1,64,32]{3,4,1,0,2:T(8,128)S(1)}, f32[8,4,1,64,32]{3,4,1,0,2:T(8,128)}, u32[]{:S(2)}, u32[]{:S(2)}) collective-permute-start(f32[8,4,1,64,32]{3,4,1,0,2:T(8,128)S(1)} %pad_maximum_fusion.34), channel_id=1, source_target_pairs={{0,1},{1,2},{2,3},{3,4},{4,5},{5,6},{6,7},{7,8},{8,9},{9,10},{10,1... | collective-permute-start | bytes 786440 | tf_op jit(solution)/shard_map/ppermute | solution.py:25
  6.2 2.4 %collective-permute-start.3 = (f32[8,4,1,64,32]{3,4,1,0,2:T(8,128)S(1)}, f32[8,4,1,64,32]{3,4,1,0,2:T(8,128)}, u32[]{:S(2)}, u32[]{:S(2)}) collective-permute-start(f32[8,4,1,64,32]{3,4,1,0,2:T(8,128)S(1)} %pad_maximum_fusion.34), channel_id=1, source_target_pairs={{1,0},{2,1},{3,2},{4,3},{5,4},{6,5},{7,6},{8,7},{9,8},{10,9},{11,1... | collective-permute-start | bytes 786440 | tf_op jit(solution)/shard_map/ppermute | solution.py:26
  8.6 0.3 copy.64
  9.0 0.3 copy.65
  9.3 1.3 %copy.62 = f32[8,1,64,64]{2,0,3,1:T(8,128)S(1)} copy(f32[8,1,64,64]{3,2,1,0:T(8,128)} %param.14) | data formatting | bytes 262144 | tf_op args[5]
  10.6 1.2 %copy.63 = f32[8,1,64,64]{2,0,3,1:T(8,128)S(1)} copy(f32[8,1,64,64]{3,2,1,0:T(8,128)} %param.15) | data formatting | bytes 262144 | tf_op args[6]
  11.8 0.1 pad_maximum_fusion.3
  12.0 0.5 copy-done.4
  12.5 1.7 %fusion.193 = (f32[8,4,1,64,64]{3,1,4,0,2:T(4,128)}, f32[8,4,1,64,64]{3,1,4,0,2:T(4,128)}) fusion(f32[8,8,1,64,64]{3,1,4,0,2:T(8,128)S(1)} %pad_maximum_fusion.3), kind=kLoop, calls=%fused_computation.355 | loop fusion | bytes 2097152 | tf_op jit(solution)/shard_map/slice | solution.py:43
  14.2 3.4 %collective-permute-start = (f32[8,4,1,64,64]{3,1,4,0,2:T(4,128)}, f32[8,4,1,64,64]{3,1,4,0,2:T(4,128)}, u32[]{:S(2)}, u32[]{:S(2)}) collective-permute-start(f32[8,4,1,64,64]{3,1,4,0,2:T(4,128)} %get-tuple-element.84), channel_id=1, source_target_pairs={{0,1},{1,2},{2,3},{4,5},{5,6},{6,7},{8,9},{9,10},{10,11},{12,13},{... | collective-permute-start | bytes 1572872 | tf_op jit(solution)/shard_map/ppermute | solution.py:42
  17.6 6.5 %collective-permute-start.1 = (f32[8,4,1,64,64]{3,1,4,0,2:T(4,128)}, f32[8,4,1,64,64]{3,1,4,0,2:T(4,128)}, u32[]{:S(2)}, u32[]{:S(2)}) collective-permute-start(f32[8,4,1,64,64]{3,1,4,0,2:T(4,128)} %get-tuple-element.85), channel_id=1, source_target_pairs={{1,0},{2,1},{3,2},{5,4},{6,5},{7,6},{9,8},{10,9},{11,10},{13,12},{... | collective-permute-start | bytes 1572872 | tf_op jit(solution)/shard_map/ppermute | solution.py:45
  24.2 0.6 compare_and_fusion.2
  24.7 0.6 compare_and_fusion
  25.3 0.5 compare_and_fusion.1
  25.9 0.5 compare_and_fusion.6
  26.8 0.6 dynamic_slice.3
  27.3 1.2 %compare_convert_fusion = (f32[2]{0:T(128)}, pred[2]{0:T(512)(128)(4,1)S(1)}) fusion(s32[]{:T(128)} %bitcast), kind=kLoop, calls=%fused_computation.347 | loop fusion | flops 6 | bytes 14 | tf_op jit(solution)/shard_map/convert_element_type | solution.py:339
  28.6 0.6 compare_and_fusion.5
  34.5 0.6 gt.46
  35.0 0.5 compare_and_fusion.3
  35.5 0.6 compare_and_fusion.4
  36.1 1.4 %pad_maximum_fusion.4 = f32[8,12,1,64,32]{3,4,1,0,2:T(8,128)S(1)} fusion(f32[8,4,1,64,32]{3,4,1,0,2:T(8,128)} %collective-permute-done.3, f32[3,4,1,64,32]{3,4,1,0,2:T(8,128)S(1)} %bitcast.106, f32[5,4,1,64,32]{3,4,1,0,2:T(8,128)S(1)} %maximum_bitcast_fusion, f32[8,4,1,64,32]{3,4,1,0,2:T(8,128)} %collective-permute-done.2), kind=kLoop, calls=%fused_computation.62 | loop fusion | flops 589824 | bytes 1572864 | tf_op jit(solution)/shard_map/concatenate | solution.py:32
  37.6 0.1 fusion.195
  37.7 1.3 %fusion.194 = (f32[1,10,1,64,32]{3,4,1,0,2:T(8,128)}, f32[10,64,32]{1,2,0:T(8,128)}, f32[1,10,1,64,32]{3,4,1,0,2:T(8,128)}, f32[10,64,32]{1,2,0:T(8,128)}, f32[1...) fusion(f32[8,12,1,64,32]{3,4,1,0,2:T(8,128)S(1)} %pad_maximum_f, ...), kind=kLoop, calls=%fused_computation.356 | loop fusion | flops 532480 | bytes 1802240 | tf_op jit(solution)/shard_map/slice | solution.py:74
  39.1 1.1 pad_slice_fusion.10
  40.2 1.5 %pad_dynamic-slice_fusion = f32[5,12,34,34]{2,3,1,0:T(8,128)} fusion(s32[]{:T(128)} %bitcast.8, f32[5,12,64,32]{2,3,1,0:T(8,128)S(1)} %get-tuple-element.97), kind=kLoop, calls=%fused_computation.68 | loop fusion | bytes 768964 | solution.py:309
  41.7 3.1 %copy.66 = f32[5,12,34,34]{3,1,2,0:T(8,128)} copy(f32[5,12,34,34]{2,3,1,0:T(8,128)} %pad_dynamic-slice_fusion) | data formatting | bytes 554880 | solution.py:309
  44.8 2.1 %broadcast_in_dim.297 = f32[5,12,2,34,34]{4,2,1,3,0:T(2,128)S(1)} broadcast(f32[5,12,34,34]{3,1,2,0:T(8,128)} %copy.66), dimensions={0,1,3,4} | broadcast | bytes 832320 | tf_op jit(solution)/shard_map/vmap()/broadcast_in_dim | solution.py:222
  46.9 2.3 %broadcast_in_dim.299 = f32[5,24,34,2,34]{4,1,3,2,0:T(8,128)} broadcast(f32[5,24,34,34]{3,1,2,0:T(8,128)S(1)} %bitcast.93), dimensions={0,1,2,4} | broadcast | bytes 1664640 | tf_op jit(solution)/shard_map/vmap()/broadcast_in_dim | solution.py:222
  49.1 5.3 %copy.67 = f32[5,24,68,34]{2,1,3,0:T(8,128)} copy(f32[5,24,68,34]{3,1,2,0:T(8,128)} %bitcast.91) | data formatting | bytes 2219520 | tf_op jit(solution)/shard_map/vmap()/broadcast_in_dim | solution.py:222
  54.4 1.9 %broadcast_in_dim.301 = f32[5,24,68,34,2]{2,1,4,3,0:T(8,128)S(1)} broadcast(f32[5,24,68,34]{2,1,3,0:T(8,128)} %copy.67), dimensions={0,1,2,3} | broadcast | bytes 3329280 | tf_op jit(solution)/shard_map/vmap()/broadcast_in_dim | solution.py:222
  56.4 0.8 slice_bitcast_fusion
  57.8 0.6 fusion.103
  58.4 0.3 select_maximum_fusion
  59.1 0.3 divide_select_fusion.1
  59.5 0.1 fusion.164
  59.7 0.2 copy-done.27
  60.0 0.7 fusion.109
  60.8 2.5 %pad_maximum_fusion = f32[8,16,1,64,64]{3,1,4,0,2:T(8,128)S(1)} fusion(f32[8,4,1,64,64]{3,1,4,0,2:T(4,128)} %collective-permute-done.1, f32[3,8,1,64,64]{3,1,4,0,2:T(8,128)S(1)} %copy-done.1, f32[1,8,1,64,64]{3,1,4,0,2:T(8,128)S(1)} %bitcast.98, f32[1,8,1,64,64]{3,1,4,0,2:T(8,128)S(1)} %bitcast.95, f32[3,8,1,64,64]{3,1,4,0,2:T(8,128)S(1)} %copy.64, ...), kind=kLoop, calls=%fused_computation | loop fusion | flops 2621440 | bytes 4194304 | tf_op jit(solution)/shard_map/concatenate | solution.py:46
  63.3 0.8 slice_select_fusion.2
  64.1 1.4 %slice_select_fusion = (f32[5,16,1,1,64]{3,1,4,0,2:T(8,128)S(1)}, f32[5,16,1,1,64]{3,1,4,0,2:T(8,128)S(1)}) fusion(f32[5,16,1,66,66]{3,1,4,0,2:T(8,128)S(1)} %slice_bitcast_fusion, f32[5,16,1,64,64]{3,1,4,0,2:T(8,128)S(1)} %slice_select_fusion.2, f32[]{:T(128)} %bitcast.20, pred[]{:T(512)} %bitcast.19, f32[]{:T(128)} %bitcast.17, pred[]{:T(512)} %bitcast.16), kind=kLoop, calls=%fused_computation.4 | loop fusion | flops 20480 | bytes 122890 | tf_op jit(solution)/shard_map/jit(_where)/select_n | solution.py:200
  65.5 3.1 %maximum_maximum_fusion = (f32[5,16,1,66,65]{3,1,4,0,2:T(8,128)S(1)}, f32[5,16,1,66,65]{3,1,4,0,2:T(8,128)S(1)}) fusion(f32[5,16,1,1,64]{3,1,4,0,2:T(8,128)S(1)} %get-tuple-element.61, f32[5,16,1,64,64]{3,1,4,0,2:T(8,128)S(1)} %slice_select_fusion.2, f32[5,16,1,1,64]{3,1,4,0,2:T(8,128)S(1)} %get-tuple-element.62, ...), kind=kLoop, calls=%fused_computation.2 | loop fusion | flops 2059200 | bytes 4139520 | tf_op jit(solution)/shard_map/concatenate | solution.py:218
  68.6 1.2 %fusion.192 = (f32[1,14,1,64,64]{3,1,4,0,2:T(8,128)S(1)}, f32[1,14,1,64,64]{3,1,4,0,2:T(8,128)S(1)}, f32[1,14,1,64,64]{3,1,4,0,2:T(8,128)S(1)}, f32[1,14,1,64,64...) fusion(f32[5,16,1,64,64]{3,1,4,0,2:T(8,128)S(1)} %slice_select_fusion.2, ...), kind=kLoop, calls=%fused_computation.354 | loop fusion | flops 745472 | bytes 12468224 | tf_op jit(solution)/shard_map/slice | solution.py:74
  69.8 1.0 multiply_bitcast_fusion.1
  71.0 4.6 %fusion.22 = f32[3,14,1,64,64]{3,1,4,0,2:T(8,128)S(1)} fusion(f32[1,14,1,64,64]{3,1,4,0,2:T(8,128)S(1)} %get-tuple-element.72, f32[1,14,1,64,64]{3,1,4,0,2:T(8,128)S(1)} %get-tuple-element.73, f32[1,14,1,64,64]{3,1,4,0,2:T(8,128)S(1)} %get-tuple-element.71, f32[5,16,1,66,65]{3,1,4,0,2:T(8,128)S(1)} %get-tuple-element.58, ...), kind=kLoop, calls=%fused_computation.63 | loop fusion | flops 5332992 | bytes 24805888 | tf_op jit(solution)/shard_map/jit(_where)/select_n | solution.py:246
  75.6 0.8 fusion.1
  76.5 4.7 %divide_select_fusion = (f32[1,12,1,64,64]{3,1,4,0,2:T(8,128)S(1)}, f32[1,12,1,64,64]{3,1,4,0,2:T(8,128)S(1)}, f32[1,12,1,64,64]{3,1,4,0,2:T(8,128)S(1)}, f32[1,...) fusion(pred[12]{0:T(512)(128)(4,1)S(1)} %copy-done.32, ...), kind=kLoop, calls=%fused_computation.186 | loop fusion | flops 3489792 | bytes 19710464 | tf_op jit(solution)/shard_map/jit(_where)/select_n | solution.py:246
  81.2 0.2 fusion.51
  81.4 0.4 copy-done.30
  81.9 1.3 %fusion.34 = f32[1,10,1,64,64]{3,1,4,0,2:T(8,128)S(1)} fusion(f32[1,12,1,64,64]{3,1,4,0,2:T(8,128)S(1)} %get-tuple-element.44, f32[1,12,1,66,1]{3,1,4,0,2:T(8,128)S(1)} %copy.74, f32[1,12,1,1,64]{3,1,4,0,2:T(8,128)S(1)} %get-tuple-element.113, f32[1,12,1,64,64]{3,1,4,0,2:T(8,128)S(1)} %get-tuple-element.42, f32[1,12,1,1,64]{3,1,4,0,2:T(8,128)S(1)} %get-tuple-element.112, ...), kind=kLoop, calls=%fused_computation.87 | loop fusion | flops 1269760 | bytes 7512576 | tf_op jit(solution)/shard_map/jit(_where)/select_n | solution.py:246
  83.2 0.2 fusion.31
  83.4 0.6 slice_subtract_fusion.11
  84.0 0.3 fusion.27
  84.3 9.2 %copy.78 = f32[4,8,1,64,64]{0,4,3,1,2:T(8,128)} copy(f32[4,8,1,64,64]{3,1,4,0,2:T(8,128)S(1)} %pad_maximum_fusion.5) | data formatting | bytes 1048576 | tf_op jit(solution)/shard_map/concatenate | solution.py:341
  93.6 12.1 %reduce_sum.8 = f32[4,4,32,32]{0,3,2,1:T(8,128)S(1)} reduce(f32[4,4,2,32,2,32,2]{0,6,5,4,3,2,1:T(2,128)} %bitcast.90, f32[]{:T(128)} %constant.81.clone.1), dimensions={2,4,6}, to_apply=%region_0.1 | reduce | flops 114688 | bytes 589828 | tf_op jit(solution)/shard_map/reduce_sum | solution.py:236
  105.7 1.0 copy.79
  106.9 0.3 multiply_bitcast_fusion
  107.2 0.3 reshape.498
  107.7 0.7 slice.1014
  108.4 0.6 slice_bitcast_fusion.1
  109.0 1.2 %copy.81 = f32[3,8,1,64,64]{4,3,2,1,0:T(8,128)} copy(f32[3,8,1,64,64]{3,1,4,0,2:T(8,128)S(1)} %fusion.27) | data formatting | bytes 786432
  110.2 0.9 copy.82
  (101 shorter events, 2.3 us)
Async XLA Ops:
  0.6 8.0 %copy-start.7 = (f32[3,8,1,64,64]{4,3,2,1,0:T(8,128)S(1)}, f32[3,8,1,64,64]{4,3,2,1,0:T(8,128)}, u32[]{:S(2)}) copy-start(f32[3,8,1,64,64]{4,3,2,1,0:T(8,128)} %param.13) | copy-start | bytes 1179652
  0.6 8.3 %copy-start.8 = (f32[3,8,1,64,64]{4,3,2,1,0:T(8,128)S(1)}, f32[3,8,1,64,64]{4,3,2,1,0:T(8,128)}, u32[]{:S(2)}) copy-start(f32[3,8,1,64,64]{4,3,2,1,0:T(8,128)} %param.16) | copy-start | bytes 1179652
  2.8 33.3 %collective-permute-start.2 = (f32[8,4,1,64,32]{3,4,1,0,2:T(8,128)S(1)}, f32[8,4,1,64,32]{3,4,1,0,2:T(8,128)}, u32[]{:S(2)}, u32[]{:S(2)}) collective-permute-start(f32[8,4,1,64,32]{3,4,1,0,2:T(8,128)S(1)} %pad_maximum_fusion.34), channel_id=1, source_target_pairs={{0,1},{1,2},{2,3},{3,4},{4,5},{5,6},{6,7},{7,8},{8,9},{9,10},{10,1... | collective-permute-start | bytes 786440 | tf_op jit(solution)/shard_map/ppermute | solution.py:25
  6.2 29.9 %collective-permute-start.3 = (f32[8,4,1,64,32]{3,4,1,0,2:T(8,128)S(1)}, f32[8,4,1,64,32]{3,4,1,0,2:T(8,128)}, u32[]{:S(2)}, u32[]{:S(2)}) collective-permute-start(f32[8,4,1,64,32]{3,4,1,0,2:T(8,128)S(1)} %pad_maximum_fusion.34), channel_id=1, source_target_pairs={{1,0},{2,1},{3,2},{4,3},{5,4},{6,5},{7,6},{8,7},{9,8},{10,9},{11,1... | collective-permute-start | bytes 786440 | tf_op jit(solution)/shard_map/ppermute | solution.py:26
  9.3 2.7 %copy-start = (f32[3,8,1,64,64]{3,1,4,0,2:T(8,128)}, f32[3,8,1,64,64]{3,1,4,0,2:T(8,128)S(1)}, u32[]{:S(2)}) copy-start(f32[3,8,1,64,64]{3,1,4,0,2:T(8,128)S(1)} %copy.65) | copy-start | bytes 1179652
  10.6 1.4 %copy-start.2 = (f32[8,1,64,64]{2,0,3,1:T(8,128)}, f32[8,1,64,64]{2,0,3,1:T(8,128)S(1)}, u32[]{:S(2)}) copy-start(f32[8,1,64,64]{2,0,3,1:T(8,128)S(1)} %copy.62) | copy-start | bytes 393220
  11.8 0.7 copy-start.4
  12.5 14.2 %copy-start.37 = (s32[64]{0:T(128)S(1)}, s32[64]{0:T(128)}, u32[]{:S(2)}) copy-start(s32[64]{0:T(128)} %param.17) | copy-start | bytes 772
  12.5 23.6 %copy-start.6 = (f32[3,4,64,32]{2,3,1,0:T(8,128)S(1)}, f32[3,4,64,32]{2,3,1,0:T(8,128)}, u32[]{:S(2)}) copy-start(f32[3,4,64,32]{2,3,1,0:T(8,128)} %param.12) | copy-start | bytes 294916
  14.2 46.5 %collective-permute-start = (f32[8,4,1,64,64]{3,1,4,0,2:T(4,128)}, f32[8,4,1,64,64]{3,1,4,0,2:T(4,128)}, u32[]{:S(2)}, u32[]{:S(2)}) collective-permute-start(f32[8,4,1,64,64]{3,1,4,0,2:T(4,128)} %get-tuple-element.84), channel_id=1, source_target_pairs={{0,1},{1,2},{2,3},{4,5},{5,6},{6,7},{8,9},{9,10},{10,11},{12,13},{... | collective-permute-start | bytes 1572872 | tf_op jit(solution)/shard_map/ppermute | solution.py:42
  17.6 43.2 %collective-permute-start.1 = (f32[8,4,1,64,64]{3,1,4,0,2:T(4,128)}, f32[8,4,1,64,64]{3,1,4,0,2:T(4,128)}, u32[]{:S(2)}, u32[]{:S(2)}) collective-permute-start(f32[8,4,1,64,64]{3,1,4,0,2:T(4,128)} %get-tuple-element.85), channel_id=1, source_target_pairs={{1,0},{2,1},{3,2},{5,4},{6,5},{7,6},{9,8},{10,9},{11,10},{13,12},{... | collective-permute-start | bytes 1572872 | tf_op jit(solution)/shard_map/ppermute | solution.py:45
  56.3 1.1 copy-start.29
  56.3 1.2 %copy-start.11 = (f32[10,64,32]{1,2,0:T(8,128)S(1)}, f32[10,64,32]{1,2,0:T(8,128)}, u32[]{:S(2)}) copy-start(f32[10,64,32]{1,2,0:T(8,128)} %get-tuple-element.87) | copy-start | bytes 245764
  56.3 1.2 %copy-start.12 = (f32[10,64,32]{1,2,0:T(8,128)S(1)}, f32[10,64,32]{1,2,0:T(8,128)}, u32[]{:S(2)}) copy-start(f32[10,64,32]{1,2,0:T(8,128)} %get-tuple-element.89) | copy-start | bytes 245764
  56.3 1.2 %copy-start.13 = (f32[10,64,32]{1,2,0:T(8,128)S(1)}, f32[10,64,32]{1,2,0:T(8,128)}, u32[]{:S(2)}) copy-start(f32[10,64,32]{1,2,0:T(8,128)} %get-tuple-element.90) | copy-start | bytes 245764
  56.3 1.2 %copy-start.14 = (f32[10,64,32]{1,2,0:T(8,128)S(1)}, f32[10,64,32]{1,2,0:T(8,128)}, u32[]{:S(2)}) copy-start(f32[10,64,32]{1,2,0:T(8,128)} %get-tuple-element.92) | copy-start | bytes 245764
  56.3 1.2 %copy-start.15 = (f32[10,64,32]{1,2,0:T(8,128)S(1)}, f32[10,64,32]{1,2,0:T(8,128)}, u32[]{:S(2)}) copy-start(f32[10,64,32]{1,2,0:T(8,128)} %get-tuple-element.93) | copy-start | bytes 245764
  56.3 1.2 %copy-start.16 = (f32[10,64,32]{1,2,0:T(8,128)S(1)}, f32[10,64,32]{1,2,0:T(8,128)}, u32[]{:S(2)}) copy-start(f32[10,64,32]{1,2,0:T(8,128)} %get-tuple-element.94) | copy-start | bytes 245764
  56.3 1.3 %copy-start.17 = (f32[10,64,32]{1,2,0:T(8,128)S(1)}, f32[10,64,32]{1,2,0:T(8,128)}, u32[]{:S(2)}) copy-start(f32[10,64,32]{1,2,0:T(8,128)} %get-tuple-element.95) | copy-start | bytes 245764
  56.3 1.3 %copy-start.18 = (f32[1,10,1,64,32]{3,4,1,0,2:T(8,128)S(1)}, f32[1,10,1,64,32]{3,4,1,0,2:T(8,128)}, u32[]{:S(2)}) copy-start(f32[1,10,1,64,32]{3,4,1,0,2:T(8,128)} %get-tuple-element.102) | copy-start | bytes 245764
  56.4 1.4 %copy-start.19 = (f32[1,10,1,64,32]{3,4,1,0,2:T(8,128)S(1)}, f32[1,10,1,64,32]{3,4,1,0,2:T(8,128)}, u32[]{:S(2)}) copy-start(f32[1,10,1,64,32]{3,4,1,0,2:T(8,128)} %get-tuple-element.103) | copy-start | bytes 245764
  56.4 1.4 %copy-start.20 = (f32[1,10,1,64,32]{3,4,1,0,2:T(8,128)S(1)}, f32[1,10,1,64,32]{3,4,1,0,2:T(8,128)}, u32[]{:S(2)}) copy-start(f32[1,10,1,64,32]{3,4,1,0,2:T(8,128)} %get-tuple-element.122) | copy-start | bytes 245764
  57.8 0.9 copy-start.21
  57.8 1.0 copy-start.22
  57.8 1.1 copy-start.23
  57.8 1.1 %copy-start.24 = (f32[1,10,1,64,32]{3,4,1,0,2:T(8,128)S(1)}, f32[1,10,1,64,32]{3,4,1,0,2:T(8,128)}, u32[]{:S(2)}) copy-start(f32[1,10,1,64,32]{3,4,1,0,2:T(8,128)} %get-tuple-element.101) | copy-start | bytes 245764
  57.8 1.2 %copy-start.25 = (f32[1,10,1,64,32]{3,4,1,0,2:T(8,128)S(1)}, f32[1,10,1,64,32]{3,4,1,0,2:T(8,128)}, u32[]{:S(2)}) copy-start(f32[1,10,1,64,32]{3,4,1,0,2:T(8,128)} %get-tuple-element.104) | copy-start | bytes 245764
  57.8 1.3 %copy-start.26 = (f32[1,10,1,64,32]{3,4,1,0,2:T(8,128)S(1)}, f32[1,10,1,64,32]{3,4,1,0,2:T(8,128)}, u32[]{:S(2)}) copy-start(f32[1,10,1,64,32]{3,4,1,0,2:T(8,128)} %get-tuple-element.105) | copy-start | bytes 245764
  57.8 1.3 %copy-start.36 = (pred[8]{0:T(512)(128)(4,1)S(1)}, pred[8]{0:T(512)(128)(4,1)}, u32[]{:S(2)}) copy-start(pred[8]{0:T(512)(128)(4,1)} %compare_and_fusion) | copy-start | bytes 28
  58.7 0.8 copy-start.33
  59.1 0.8 copy-start.27
  59.1 1.0 copy-start.9
  59.4 1.4 %copy-start.1 = (f32[3,8,1,64,64]{3,1,4,0,2:T(8,128)S(1)}, f32[3,8,1,64,64]{3,1,4,0,2:T(8,128)}, u32[]{:S(2)}) copy-start(f32[3,8,1,64,64]{3,1,4,0,2:T(8,128)} %copy-done) | copy-start | bytes 1179652
  59.4 1.4 %copy-start.3 = (f32[8,1,64,64]{2,0,3,1:T(8,128)S(1)}, f32[8,1,64,64]{2,0,3,1:T(8,128)}, u32[]{:S(2)}) copy-start(f32[8,1,64,64]{2,0,3,1:T(8,128)} %copy-done.2) | copy-start | bytes 393220
  59.4 1.4 %copy-start.5 = (f32[8,1,64,64]{2,0,3,1:T(8,128)S(1)}, f32[8,1,64,64]{2,0,3,1:T(8,128)}, u32[]{:S(2)}) copy-start(f32[8,1,64,64]{2,0,3,1:T(8,128)} %copy-done.4) | copy-start | bytes 393220
  60.8 2.5 %copy-start.31 = (pred[16]{0:T(512)(128)(4,1)S(1)}, pred[16]{0:T(512)(128)(4,1)}, u32[]{:S(2)}) copy-start(pred[16]{0:T(512)(128)(4,1)} %compare_and_fusion.6) | copy-start | bytes 52
  69.8 1.0 copy-start.28
  75.6 0.8 copy-start.32
  81.2 0.7 copy-start.30
  105.7 1.2 %copy-start.34 = (f32[2]{0:T(128)S(1)}, f32[2]{0:T(128)}, u32[]{:S(2)}) copy-start(f32[2]{0:T(128)} %get-tuple-element.120) | copy-start | bytes 28
  105.7 1.8 %copy-start.35 = (pred[64]{0:T(512)(128)(4,1)S(1)}, pred[64]{0:T(512)(128)(4,1)}, u32[]{:S(2)}) copy-start(pred[64]{0:T(512)(128)(4,1)} %gt.46) | copy-start | bytes 196
  106.7 0.9 copy-start.10
where the time goes:
time: 112 us; the launch traced here: 111 us
  other arithmetic  49.3 us (44%)
  local copies, waits for them, and re-layouts  39.4 us (35%)
  starting transfers between devices  15.8 us (14%)
  between operations  6.64 us (6%)
    reduce_sum x1, other arithmetic, coarsen(): return 0.125 * jnp.sum(shaped, axis=(2, 5, 7))  12.1 us
    select_n x8, other arithmetic, fix_planes(): jnp.where(plane_valid(field_in.shape[1], base, limit, inner), field_in, 0.0)  12 us
    concatenate x1, local copies, waits for them, and re-layouts, on_device(): averaged = coarsen(jnp.concatenate([fine_vel_new, fine_pres_new], 0))  9.24 us
    broadcast_in_dim x2, local copies, waits for them, and re-layouts, upsample(): jnp.repeat(jnp.repeat(coarse_block, 2, axis=1), 2, axis=2)  7.52 us
    unnamed x82, local copies, waits for them, and re-layouts  7.21 us
    ppermute x1, starting transfers between devices, with_halo(): lax.ppermute(lax.slice_in_dim(block, 0, width, axis=dim), axis, backward)  6.52 us
    another operation x2, local copies, waits for them, and re-layouts, inject_one(): lax.dynamic_slice(coarse_pad, (jnp.int32(0), jnp.int32(0), start_y, start...  4.64 us
    and x7, other arithmetic, plane_valid(): return ((index_all >= 0) & (index_all < limit))[None, :, None, None, None]  3.9 us
  transfers between devices with their start and end apart: 4, of which 0 were waited for; matrix products, arithmetic and copies ran while one was open for 32% of the time, Pallas kernels for 0%

commit v1 on v0

v1 whole, which is shorter than its diff:
```python
import functools

import jax
import jax.numpy as jnp
from jax import lax
from jax.experimental import pallas as pl
from jax.experimental.pallas import tpu as pltpu
from jax.sharding import PartitionSpec as P

MESH = pl.DeviceIdType.MESH
F32 = jnp.float32
BF16 = jnp.bfloat16

HALF = 64
LANES = 128
TOP = 8

FN, FR = 8, 32
CN, CR = 4, 16

UZ, UR, UL, PR, MU, TZ, TR, DA, U1, U2 = range(10)
TL, RI, RV, VF = 0, 1, 2, 3


def lane_of(rows):
    return lax.broadcasted_iota(jnp.int32, (rows, LANES), 1)


def split3(x):
    hi = x.astype(BF16)
    rest = x - hi.astype(F32)
    mid = rest.astype(BF16)
    low = (rest - mid.astype(F32)).astype(BF16)
    return hi, mid, low


def pick_nt(sel, data):
    dims = (((1,), (1,)), ((), ()))
    return sum(
        lax.dot_general(sel, part, dims, preferred_element_type=F32) for part in split3(data)
    )


def pick_nn(data, sel):
    dims = (((1,), (0,)), ((), ()))
    return sum(
        lax.dot_general(part, sel, dims, preferred_element_type=F32) for part in split3(data)
    )


def one_where(cond):
    return jnp.where(cond, 1.0, 0.0).astype(BF16)


class Level:
    def __init__(self, planes, rows, inv_sq, inv_two, pad, flat):
        self.n, self.rows, self.inv_sq, self.inv_two = planes, rows, inv_sq, inv_two
        self.pad, self.flat = pad, flat
        lane = lane_of(rows) % HALF
        self.first = lane == 0
        self.last = lane == HALF - 1

    def mid(self, slot, z):
        return self.pad[slot, z, TOP : TOP + self.rows, :]

    def row_dn(self, slot, z):
        return self.pad[slot, z, TOP - 1 : TOP - 1 + self.rows, :]

    def row_up(self, slot, z):
        return self.pad[slot, z, TOP + 1 : TOP + 1 + self.rows, :]

    def lane_dn(self, x):
        return jnp.where(self.first, 0.0, pltpu.roll(x, 1, 1))

    def lane_up(self, x):
        return jnp.where(self.last, 0.0, pltpu.roll(x, LANES - 1, 1))

    def put(self, slot, z, x, ghost_lo=0.0, ghost_hi=0.0):
        self.pad[slot, z, TOP : TOP + self.rows, :] = x
        left = lane_of(1) < HALF
        head = pltpu.roll(x[0:1], HALF, 1)
        tail = pltpu.roll(x[self.rows - 1 : self.rows], HALF, 1)
        self.pad[slot, z, TOP - 1 : TOP, :] = jnp.where(left, ghost_lo, tail)
        self.pad[slot, z, TOP + self.rows : TOP + self.rows + 1, :] = jnp.where(
            left, head, ghost_hi
        )

    def around(self, slot, z):
        x = self.mid(slot, z)
        return x, [
            self.mid(slot, z - 1),
            self.mid(slot, z + 1),
            self.row_dn(slot, z),
            self.row_up(slot, z),
            self.lane_dn(x),
            self.lane_up(x),
        ]

    def relax(self, z, force):
        mu, nb = self.around(MU, z)
        sums = [mu + m for m in nb]
        total = (sums[0] + sums[1]) + (sums[2] + sums[3]) + (sums[4] + sums[5])
        half = 0.5 * self.inv_sq
        diag = (1.25 * half) * total
        inv = 1.0 / diag
        _, pres = self.around(PR, z)
        out = []
        for comp, slot in enumerate((UZ, UR, UL)):
            u, nb = self.around(slot, z)
            acc = functools.reduce(lambda a, b: a + b, [s * v for s, v in zip(sums, nb)])
            grad = self.inv_two * (pres[2 * comp + 1] - pres[2 * comp])
            out.append(0.2 * u + (force[comp] - grad + half * acc) * inv)
        self.pad[TZ, z, TOP : TOP + self.rows, :] = out[0]
        rows = self.rows
        self.put(
            TR,
            z,
            out[1],
            self.pad[UR, z, TOP - 1 : TOP, :],
            self.pad[UR, z, TOP + rows : TOP + rows + 1, :],
        )
        self.put(DA, z, diag)
        self.flat[TL, z] = out[2]
        self.flat[RI, z] = inv

    def first_update(self, z):
        tl = self.flat[TL, z]
        div = (
            (self.mid(TZ, z + 1) - self.mid(TZ, z - 1))
            + (self.row_up(TR, z) - self.row_dn(TR, z))
            + (self.lane_up(tl) - self.lane_dn(tl))
        )
        diag, nb = self.around(DA, z)
        faces = [1.0 / (diag + d) for d in nb]
        inv = 1.0 / ((faces[0] + faces[1]) + (faces[2] + faces[3]) + (faces[4] + faces[5]))
        for i, face in enumerate(faces):
            self.flat[VF + i, z] = face
        self.flat[RV, z] = inv
        self.put(U1, z, (-0.4 * self.inv_two / self.inv_sq) * div * inv)

    def sweep(self, z):
        u, nb = self.around(U1, z)
        acc = functools.reduce(
            lambda a, b: a + b, [self.flat[VF + i, z] * v for i, v in enumerate(nb)]
        )
        self.put(U2, z, 1.2 * u + (0.8 * self.flat[RV, z]) * acc)

    def finish(self, z):
        u, nb = self.around(U2, z)
        inv = self.inv_two * self.flat[RI, z]
        tees = (self.mid(TZ, z), self.mid(TR, z), self.flat[TL, z])
        vel = [t - (nb[2 * i + 1] - nb[2 * i]) * inv for i, t in enumerate(tees)]
        return vel, self.mid(PR, z) + u


def packed(raw, rows):
    return jnp.concatenate([raw[0:rows], raw[rows : 2 * rows]], axis=1)


def smooth_kernel(
    groups,
    subs,
    spots,
    cu_hbm,
    cp_hbm,
    cm_hbm,
    cf_hbm,
    fu_hbm,
    fp_hbm,
    fm_hbm,
    ff_hbm,
    fine_out,
    coarse_out,
    cu,
    cp,
    cm,
    cf,
    fu,
    fp,
    fm,
    ff,
    fpad,
    fflat,
    cpad,
    cflat,
    sb1,
    rb1,
    sb2,
    rb2,
    sb3,
    rb3,
    sb4,
    rb4,
    in_sem,
    send_sem,
    recv_sem,
):
    g = lax.axis_index("boxgrp")
    s = lax.axis_index("sub")
    up = (lax.rem(g + (s + 1) // subs, groups), lax.rem(s + 1, subs))
    down = (
        lax.rem(g + (groups - 1) + (s + subs - 1) // subs, groups),
        lax.rem(s + subs - 1, subs),
    )
    dev = g * subs + s
    at_low = dev == 0
    at_high = dev == groups * subs - 1
    box_low = s == 0
    box_high = s == subs - 1

    barrier = pltpu.get_barrier_semaphore()
    for neighbour in (up, down):
        pl.semaphore_signal(barrier, inc=1, device_id=neighbour, device_id_type=MESH)

    loads = []

    def load(src, dst):
        copy = pltpu.make_async_copy(src, dst, in_sem.at[len(loads)])
        copy.start()
        loads.append(copy)

    for src, dst in ((cu_hbm, cu), (cp_hbm, cp), (cm_hbm, cm)):
        load(src, dst)
    load(fu_hbm, fu)
    load(fp_hbm, fp)
    load(fm_hbm, fm)
    load(cf_hbm, cf)
    load(ff_hbm, ff)

    fine = Level(FN, FR, 4.0, 1.0, fpad, fflat)
    coarse = Level(CN, CR, 1.0, 0.5, cpad, cflat)

    for copy in loads[0:3]:
        copy.wait()

    def coarse_raw(slot, k):
        if slot == UZ:
            return cu[0, k]
        if slot == UR:
            return cu[2, k]
        if slot == UL:
            return cu[1, k]
        return cp[k] if slot == PR else cm[k]

    for k in range(CN):
        for slot in range(5):
            coarse.put(slot, k + 1, packed(coarse_raw(slot, k), CR))

    def for_fine(slot, k):
        if slot < PR:
            return cu[slot, k]
        return cp[k] if slot == PR else cm[k]

    edge = jnp.where(box_high, CN - 1, 0)
    q_edge = jnp.where(
        box_high, spots[lax.rem(g + 1, groups)], spots[lax.rem(g + groups - 1, groups)]
    )
    q_edge = jnp.maximum(q_edge, 0)
    row = lax.broadcasted_iota(jnp.int32, (2 * FR, HALF), 0)
    col = lax.broadcasted_iota(jnp.int32, (2 * FR, HALF), 1)
    pick_y = one_where(col == 32 * q_edge + row // 2)
    row = lax.broadcasted_iota(jnp.int32, (32, LANES), 0)
    col = lax.broadcasted_iota(jnp.int32, (32, LANES), 1)
    pick_x = one_where(row == (col % HALF) // 2)
    ghost = []
    for slot in range(5):
        plane = jnp.where(box_high, for_fine(slot, CN - 1), for_fine(slot, 0))
        ghost.append(pick_nt(pick_y, plane))
    ghost = pick_nn(jnp.concatenate(ghost, axis=0), pick_x)
    left = lane_of(FR) < HALF
    ghost = [
        jnp.where(left, ghost[64 * i : 64 * i + 32], ghost[64 * i + 32 : 64 * i + 64])
        for i in range(5)
    ]

    q_own = spots[g]
    col = lax.broadcasted_iota(jnp.int32, (16, HALF), 1)
    pick_row = one_where(col == jnp.where(q_own == 1, 31, 32))
    rows = []
    for slot in range(5):
        planes = jnp.concatenate([for_fine(slot, k) for k in range(CN)], axis=0)
        rows.append(pick_nt(pick_row, planes))
    row = lax.broadcasted_iota(jnp.int32, (LANES, CN * LANES), 0)
    col = lax.broadcasted_iota(jnp.int32, (LANES, CN * LANES), 1)
    pick_k = one_where(row == 32 * (col // LANES) + (col % HALF) // 2)
    rows = pick_nn(jnp.concatenate(rows, axis=0), pick_k)

    def fine_raw(slot, z):
        if slot < PR:
            return fu[slot, z]
        return fp[z] if slot == PR else fm[z]

    for copy in loads[3:6]:
        copy.wait()
    for z in range(FN):
        for slot in range(5):
            k = z // 2
            line = rows[16 * slot : 16 * slot + 1, LANES * k : LANES * (k + 1)]
            lo = jnp.where(q_own == 1, line, 0.0)
            hi = jnp.where(q_own == 1, 0.0, line)
            fine.put(slot, z + 1, packed(fine_raw(slot, z), FR), lo, hi)

    for slot in range(5):
        at = slice(slot * FR, (slot + 1) * FR)
        sb1[0, at, :] = jnp.where(box_high, ghost[slot], fine.mid(slot, FN))
        sb1[1, at, :] = jnp.where(box_low, ghost[slot], fine.mid(slot, 1))
        at = slice(5 * FR + slot * CR, 5 * FR + (slot + 1) * CR)
        sb1[0, at, :] = coarse.mid(slot, CN)
        sb1[1, at, :] = coarse.mid(slot, 1)

    sends = []

    def exchange(sb, rb):
        pair = []
        for side, device in enumerate((up, down)):
            i = len(sends)
            copy = pltpu.make_async_remote_copy(
                src_ref=sb.at[side],
                dst_ref=rb.at[side],
                send_sem=send_sem.at[i],
                recv_sem=recv_sem.at[i],
                device_id=device,
                device_id_type=MESH,
            )
            copy.start()
            sends.append(copy)
            pair.append(copy)
        return pair

    def arrive(pair):
        for copy in pair:
            copy.wait_recv()

    def both(fine_step, coarse_step):
        @pl.loop(2, FN)
        def _(z):
            fine_step(z)

        @pl.loop(2, CN)
        def _(z):
            coarse_step(z)

    def ends(fine_step, coarse_step):
        for z in (1, FN):
            fine_step(z)
        for z in (1, CN):
            coarse_step(z)

    def fine_relax(z):
        fine.relax(z, [packed(ff[c, z - 1], FR) for c in range(3)])

    def coarse_relax(z):
        coarse.relax(z, [packed(cf[c, z - 1], CR) for c in (0, 2, 1)])

    pl.semaphore_wait(barrier, 2)
    pair = exchange(sb1, rb1)
    for copy in loads[6:8]:
        copy.wait()
    both(fine_relax, coarse_relax)
    arrive(pair)
    for slot in range(5):
        for side, out_side, z in ((0, at_low, 0), (1, at_high, FN + 1)):
            value = rb1[side, slot * FR : (slot + 1) * FR, :]
            fpad[slot, z, TOP : TOP + FR, :] = jnp.where(out_side, 0.0, value)
        for side, out_side, z in ((0, at_low, 0), (1, at_high, CN + 1)):
            value = rb1[side, 5 * FR + slot * CR : 5 * FR + (slot + 1) * CR, :]
            cpad[slot, z, TOP : TOP + CR, :] = jnp.where(out_side, 0.0, value)
    ends(fine_relax, coarse_relax)

    for side, zf, zc in ((0, FN, CN), (1, 1, 1)):
        sb2[side, 0:32, :] = fine.mid(TZ, zf)
        sb2[side, 32:64, :] = fine.mid(DA, zf)
        sb2[side, 64:80, :] = coarse.mid(TZ, zc)
        sb2[side, 80:96, :] = coarse.mid(DA, zc)
    pair = exchange(sb2, rb2)
    both(fine.first_update, coarse.first_update)
    arrive(pair)
    for side, box_side, out_side, zf, zc in (
        (0, box_low, at_low, 0, 0),
        (1, box_high, at_high, FN + 1, CN + 1),
    ):
        at = slice(TOP, TOP + FR)
        fpad[TZ, zf, at, :] = jnp.where(box_side, fpad[UZ, zf, at, :], rb2[side, 0:32, :])
        fpad[DA, zf, at, :] = jnp.where(box_side, 0.0, rb2[side, 32:64, :])
        at = slice(TOP, TOP + CR)
        cpad[TZ, zc, at, :] = jnp.where(out_side, 0.0, rb2[side, 64:80, :])
        cpad[DA, zc, at, :] = jnp.where(out_side, 0.0, rb2[side, 80:96, :])
    ends(fine.first_update, coarse.first_update)

    def swap_update(slot, sb, rb, fine_step, coarse_step):
        for side, zf, zc in ((0, FN, CN), (1, 1, 1)):
            sb[side, 0:32, :] = fine.mid(slot, zf)
            sb[side, 32:48, :] = coarse.mid(slot, zc)
        pair = exchange(sb, rb)
        both(fine_step, coarse_step)
        arrive(pair)
        for side, box_side, out_side, zf, zc in (
            (0, box_low, at_low, 0, 0),
            (1, box_high, at_high, FN + 1, CN + 1),
        ):
            fpad[slot, zf, TOP : TOP + FR, :] = jnp.where(box_side, 0.0, rb[side, 0:32, :])
            cpad[slot, zc, TOP : TOP + CR, :] = jnp.where(out_side, 0.0, rb[side, 32:48, :])
        ends(fine_step, coarse_step)

    def fine_finish(z):
        vel, pres = fine.finish(z)
        for i in range(3):
            fine_out[i, z - 1] = vel[i]
        fine_out[3, z - 1] = pres

    def coarse_finish(z):
        vel, pres = coarse.finish(z)
        for i, c in enumerate((0, 2, 1)):
            coarse_out[c, z - 1] = vel[i]
        coarse_out[3, z - 1] = pres

    swap_update(U1, sb3, rb3, fine.sweep, coarse.sweep)
    swap_update(U2, sb4, rb4, fine_finish, coarse_finish)
    for copy in sends:
        copy.wait_send()


def place_kernel(spots, fine_in, coarse_in, fvel, fpres, cvel, cpres):
    q = spots[lax.axis_index("boxgrp")]
    filled = q >= 0
    dims = (((1,), (1,)), ((), ()))
    pairs = []
    for f in range(4):
        for k in range(CN):
            for z in (2 * k, 2 * k + 1):
                x = jnp.where(filled, fine_in[f, z], 0.0)
                for half in range(2):
                    piece = x[:, half * HALF : (half + 1) * HALF]
                    at = slice(half * FR, (half + 1) * FR)
                    if f < 3:
                        fvel[f, z, at, :] = piece
                    else:
                        fpres[z, at, :] = piece
            ref = fvel.at[f] if f < 3 else fpres
            total = None
            for z in (2 * k, 2 * k + 1):
                for start in range(2):
                    part = ref[z, pl.ds(start, FR, stride=2), :]
                    total = part if total is None else total + part
            pairs.append(total)
    row = lax.broadcasted_iota(jnp.int32, (32, HALF), 0)
    col = lax.broadcasted_iota(jnp.int32, (32, HALF), 1)
    mean = jnp.where(row == col // 2, 0.125, 0.0).astype(BF16)
    lane = lane_of(32)
    for f in range(4):
        blk = pick_nt(mean, jnp.concatenate(pairs[4 * f : 4 * f + 4], axis=0))
        for k in range(CN):
            lo = pltpu.roll(blk, (LANES - 32 * k) % LANES, 1) if k else blk
            hi = pltpu.roll(blk, (LANES + 32 - 32 * k) % LANES, 1) if k != 1 else blk
            covered = jnp.where(lane < 32, lo, hi)[:, 0:HALF]
            x = coarse_in[f, k]
            own = jnp.concatenate([x[:, 0:HALF], x[:, HALF:LANES]], axis=0)
            value = jnp.where(lane[:, 0:HALF] // 32 == q, covered, own)
            if f < 3:
                cvel[f, k] = value
            else:
                cpres[k] = value


def on_device(groups, subs, cu, cp, cm, cf, fu, fp, fm, ff, spots):
    cu, cf = [a.transpose(0, 1, 3, 2) for a in (cu, cf)]
    cp, cm = [a.transpose(0, 2, 1) for a in (cp, cm)]
    fu, ff = [a[:, :, 0] for a in (fu, ff)]
    fp, fm = [a[:, 0] for a in (fp, fm)]
    vmem = functools.partial(pltpu.VMEM, dtype=F32)
    smem_spec = pl.BlockSpec(memory_space=pltpu.SMEM)
    any_spec = pl.BlockSpec(memory_space=pl.ANY)
    vmem_spec = pl.BlockSpec(memory_space=pltpu.VMEM)
    fine, coarse = pl.pallas_call(
        functools.partial(smooth_kernel, groups, subs),
        out_shape=(
            jax.ShapeDtypeStruct((4, FN, FR, LANES), F32),
            jax.ShapeDtypeStruct((4, CN, CR, LANES), F32),
        ),
        in_specs=[smem_spec] + [any_spec] * 8,
        out_specs=(vmem_spec, vmem_spec),
        scratch_shapes=[vmem(a.shape) for a in (cu, cp, cm, cf, fu, fp, fm, ff)]
        + [
            vmem((10, FN + 2, FR + 16, LANES)),
            vmem((9, FN + 2, FR, LANES)),
            vmem((10, CN + 2, CR + 16, LANES)),
            vmem((9, CN + 2, CR, LANES)),
        ]
        + [vmem((2, r * (FR + CR), LANES)) for r in (5, 5, 2, 2, 1, 1, 1, 1)]
        + [
            pltpu.SemaphoreType.DMA((8,)),
            pltpu.SemaphoreType.DMA((8,)),
            pltpu.SemaphoreType.DMA((8,)),
        ],
        compiler_params=pltpu.CompilerParams(
            collective_id=0, has_side_effects=True, vmem_limit_bytes=32 * 1024 * 1024
        ),
        name="smooth",
    )(spots, cu, cp, cm, cf, fu, fp, fm, ff)
    fvel, fpres, cvel, cpres = pl.pallas_call(
        place_kernel,
        out_shape=tuple(jax.ShapeDtypeStruct(a.shape, F32) for a in (fu, fp, cu, cp)),
        in_specs=[smem_spec, vmem_spec, vmem_spec],
        out_specs=(vmem_spec,) * 4,
        compiler_params=pltpu.CompilerParams(vmem_limit_bytes=16 * 1024 * 1024),
        name="place",
    )(spots, fine, coarse)
    return (
        cvel.transpose(0, 1, 3, 2),
        cpres.transpose(0, 2, 1),
        fvel[:, :, None],
        fpres[:, None],
    )


def solution(mesh):
    groups, subs = mesh.shape["boxgrp"], mesh.shape["sub"]
    zs = ("boxgrp", "sub")
    return jax.shard_map(
        functools.partial(on_device, groups, subs),
        mesh=mesh,
        in_specs=(
            P(None, zs, None, None),
            P(zs, None, None),
            P(zs, None, None),
            P(None, zs, None, None),
            P(None, "sub", "boxgrp", None, None),
            P("sub", "boxgrp", None, None),
            P("sub", "boxgrp", None, None),
            P(None, "sub", "boxgrp", None, None),
            P(),
        ),
        out_specs=(
            P(None, zs, None, None),
            P(zs, None, None),
            P(None, "sub", "boxgrp", None, None),
            P("sub", "boxgrp", None, None),
        ),
        check_vma=False,
    )
```

time: 112 us -> 42.6 us (0.38)
  the two profiles are of different devices: /device:TPU:130 before, /device:TPU:0 now
where the time goes in v1:
time: 42.6 us; the launch traced here: 42.3 us
  Pallas kernels  33.3 us (78%)
  local copies, waits for them, and re-layouts  8.34 us (20%)
  between operations  0.66 us (2%)
    pallas_call x1, Pallas kernels, on_device(): pl.pallas_call(functools.partial(smooth_kernel, groups, subs), out_shape=...  31.4 us
    unnamed x18, local copies, waits for them, and re-layouts  8.34 us
    pallas_call x1, Pallas kernels, on_device(): pl.pallas_call(place_kernel, out_shape=tuple((jax.ShapeDtypeStruct(a.shap...  1.84 us

profile of v1, /device:TPU:0, one launch (start us, length us, event | category | flops | bytes accessed | tf_op | source)
XLA Modules:
  0.0 42.3 jit_solution(4841882853280986176)
XLA Ops:
  0.6 0.0 copy-start.8
  0.6 0.6 %copy-done.8 = s32[64]{0:T(128)S(1)} copy-done((s32[64]{0:T(128)S(1)}, s32[64]{0:T(128)}, u32[]{:S(2)}) %copy-start.8) | copy-done | bytes 280
  1.3 0.0 copy-start
  1.3 1.1 %copy-done = f32[3,8,1,64,64]{4,3,2,1,0:T(8,128)S(1)} copy-done((f32[3,8,1,64,64]{4,3,2,1,0:T(8,128)S(1)}, f32[3,8,1,64,64]{4,3,2,1,0:T(8,128)}, u32[]{:S(2)}) %copy-start) | copy-done | bytes 393240
  2.4 0.0 copy-start.1
  2.4 1.1 %copy-done.1 = f32[3,8,1,64,64]{4,3,2,1,0:T(8,128)S(1)} copy-done((f32[3,8,1,64,64]{4,3,2,1,0:T(8,128)S(1)}, f32[3,8,1,64,64]{4,3,2,1,0:T(8,128)}, u32[]{:S(2)}) %copy-start.1) | copy-done | bytes 393240
  3.6 0.0 copy-start.2
  3.6 0.9 %copy-done.2 = f32[8,1,64,64]{3,2,1,0:T(8,128)S(1)} copy-done((f32[8,1,64,64]{3,2,1,0:T(8,128)S(1)}, f32[8,1,64,64]{3,2,1,0:T(8,128)}, u32[]{:S(2)}) %copy-start.2) | copy-done | bytes 131096
  4.5 0.0 copy-start.3
  4.5 0.9 %copy-done.3 = f32[8,1,64,64]{3,2,1,0:T(8,128)S(1)} copy-done((f32[8,1,64,64]{3,2,1,0:T(8,128)S(1)}, f32[8,1,64,64]{3,2,1,0:T(8,128)}, u32[]{:S(2)}) %copy-start.3) | copy-done | bytes 131096
  5.5 0.0 copy-start.4
  5.5 0.9 %copy-done.4 = f32[3,4,64,32]{2,3,1,0:T(8,128)S(1)} copy-done((f32[3,4,64,32]{2,3,1,0:T(8,128)S(1)}, f32[3,4,64,32]{2,3,1,0:T(8,128)}, u32[]{:S(2)}) %copy-start.4) | copy-done | bytes 98328
  6.4 0.0 copy-start.5
  6.4 0.9 %copy-done.5 = f32[3,4,64,32]{2,3,1,0:T(8,128)S(1)} copy-done((f32[3,4,64,32]{2,3,1,0:T(8,128)S(1)}, f32[3,4,64,32]{2,3,1,0:T(8,128)}, u32[]{:S(2)}) %copy-start.5) | copy-done | bytes 98328
  7.3 0.0 copy-start.6
  7.3 0.8 %copy-done.6 = f32[4,64,32]{1,2,0:T(8,128)S(1)} copy-done((f32[4,64,32]{1,2,0:T(8,128)S(1)}, f32[4,64,32]{1,2,0:T(8,128)}, u32[]{:S(2)}) %copy-start.6) | copy-done | bytes 32792
  8.2 0.0 copy-start.7
  8.2 0.8 %copy-done.7 = f32[4,64,32]{1,2,0:T(8,128)S(1)} copy-done((f32[4,64,32]{1,2,0:T(8,128)S(1)}, f32[4,64,32]{1,2,0:T(8,128)}, u32[]{:S(2)}) %copy-start.7) | copy-done | bytes 32792
  9.0 31.4 %smooth.1 = (f32[4,8,32,128]{3,2,1,0:T(8,128)S(1)}, f32[4,4,16,128]{3,2,1,0:T(8,128)S(1)}) custom-call(s32[64]{0:T(128)S(1)} %copy-done.8, f32[3,4,32,64]{3,2,1,0:T(8,128)S(1)} %bitcast.20, f32[4,32,64]{2,1,0:T(8,128)S(1)} %bitcast.22, f32[4,32,64]{2,1,0:T(8,128)S(1)} %bitcast.23, f32[3,4,32,64]{3,2,1,0:T(8,128)S(1)} %bitcast.21, ...), custom_call_target="tpu_custom_call" | custom-call | tf_op jit(solution)/shard_map/smooth/pallas_call | solution.py:474
  40.4 1.8 %place.1 = (f32[3,8,64,64]{3,2,1,0:T(8,128)}, f32[8,64,64]{2,1,0:T(8,128)}, f32[3,4,32,64]{3,2,1,0:T(8,128)}, f32[4,32,64]{2,1,0:T(8,128)}) custom-call(s32[64]{0:T(128)S(1)} %copy-done.8, f32[4,8,32,128]{3,2,1,0:T(8,128)S(1)} %get-tuple-element.10.fine_in, f32[4,4,16,128]{3,2,1,0:T(8,128)S(1)} %get-tuple-element.11.coarse_in), custom_call_target="tpu_custom_call" | custom-call | tf_op jit(solution)/shard_map/place/pallas_call | solution.py:500
Async XLA Ops:
  0.6 0.7 %copy-start.8 = (s32[64]{0:T(128)S(1)}, s32[64]{0:T(128)}, u32[]{:S(2)}) copy-start(s32[64]{0:T(128)} %spots.3) | copy-start | bytes 772
  1.3 1.1 %copy-start = (f32[3,8,1,64,64]{4,3,2,1,0:T(8,128)S(1)}, f32[3,8,1,64,64]{4,3,2,1,0:T(8,128)}, u32[]{:S(2)}) copy-start(f32[3,8,1,64,64]{4,3,2,1,0:T(8,128)} %param.13) | copy-start | bytes 1179652
  2.4 1.1 %copy-start.1 = (f32[3,8,1,64,64]{4,3,2,1,0:T(8,128)S(1)}, f32[3,8,1,64,64]{4,3,2,1,0:T(8,128)}, u32[]{:S(2)}) copy-start(f32[3,8,1,64,64]{4,3,2,1,0:T(8,128)} %param.16) | copy-start | bytes 1179652
  3.6 0.9 %copy-start.2 = (f32[8,1,64,64]{3,2,1,0:T(8,128)S(1)}, f32[8,1,64,64]{3,2,1,0:T(8,128)}, u32[]{:S(2)}) copy-start(f32[8,1,64,64]{3,2,1,0:T(8,128)} %param.14) | copy-start | bytes 393220
  4.5 0.9 %copy-start.3 = (f32[8,1,64,64]{3,2,1,0:T(8,128)S(1)}, f32[8,1,64,64]{3,2,1,0:T(8,128)}, u32[]{:S(2)}) copy-start(f32[8,1,64,64]{3,2,1,0:T(8,128)} %param.15) | copy-start | bytes 393220
  5.5 0.9 %copy-start.4 = (f32[3,4,64,32]{2,3,1,0:T(8,128)S(1)}, f32[3,4,64,32]{2,3,1,0:T(8,128)}, u32[]{:S(2)}) copy-start(f32[3,4,64,32]{2,3,1,0:T(8,128)} %param.9) | copy-start | bytes 294916
  6.4 0.9 %copy-start.5 = (f32[3,4,64,32]{2,3,1,0:T(8,128)S(1)}, f32[3,4,64,32]{2,3,1,0:T(8,128)}, u32[]{:S(2)}) copy-start(f32[3,4,64,32]{2,3,1,0:T(8,128)} %param.12) | copy-start | bytes 294916
  7.3 0.8 %copy-start.6 = (f32[4,64,32]{1,2,0:T(8,128)S(1)}, f32[4,64,32]{1,2,0:T(8,128)}, u32[]{:S(2)}) copy-start(f32[4,64,32]{1,2,0:T(8,128)} %param.10) | copy-start | bytes 98308
  8.2 0.8 %copy-start.7 = (f32[4,64,32]{1,2,0:T(8,128)S(1)}, f32[4,64,32]{1,2,0:T(8,128)}, u32[]{:S(2)}) copy-start(f32[4,64,32]{1,2,0:T(8,128)} %param.11) | copy-start | bytes 98308

commit v2 on v1

v2 whole, which is shorter than its diff:
```python
import functools

import jax
import jax.numpy as jnp
from jax import lax
from jax.experimental import pallas as pl
from jax.experimental.pallas import tpu as pltpu
from jax.sharding import PartitionSpec as P

MESH = pl.DeviceIdType.MESH
F32 = jnp.float32
BF16 = jnp.bfloat16

HALF = 64
LANES = 128
TOP = 8

FN, FR = 8, 32
CN, CR = 4, 16

OFF = 4
DEEP = 4

UZ, UR, UL, PR, MU, TZ, TR, DA, U1, U2 = range(10)
TL, RI, RV, S0, F0, F1, F2, VF = 0, 1, 2, 3, 4, 5, 6, 7
FLAT = VF + 6

COARSE_MSG = (
    (UZ, True, 4),
    (PR, True, 4),
    (MU, True, 4),
    (UR, True, 3),
    (UL, True, 3),
    (F0, False, 3),
    (F1, False, 2),
    (F2, False, 2),
)
COARSE_ROWS = CR * sum(depth for _, _, depth in COARSE_MSG)


def lane_of(rows):
    return lax.broadcasted_iota(jnp.int32, (rows, LANES), 1)


def split3(x):
    hi = x.astype(BF16)
    rest = x - hi.astype(F32)
    mid = rest.astype(BF16)
    low = (rest - mid.astype(F32)).astype(BF16)
    return hi, mid, low


def pick_nt(sel, data):
    dims = (((1,), (1,)), ((), ()))
    return sum(
        lax.dot_general(sel, part, dims, preferred_element_type=F32) for part in split3(data)
    )


def pick_nn(data, sel):
    dims = (((1,), (0,)), ((), ()))
    return sum(
        lax.dot_general(part, sel, dims, preferred_element_type=F32) for part in split3(data)
    )


def one_where(cond):
    return jnp.where(cond, 1.0, 0.0).astype(BF16)


class Level:
    def __init__(self, planes, rows, inv_sq, inv_two, pad, flat):
        self.n, self.rows, self.inv_sq, self.inv_two = planes, rows, inv_sq, inv_two
        self.pad, self.flat = pad, flat
        lane = lane_of(rows) % HALF
        self.first = lane == 0
        self.last = lane == HALF - 1

    def mid(self, slot, z):
        return self.pad[slot, z + OFF, TOP : TOP + self.rows, :]

    def row_dn(self, slot, z):
        return self.pad[slot, z + OFF, TOP - 1 : TOP - 1 + self.rows, :]

    def row_up(self, slot, z):
        return self.pad[slot, z + OFF, TOP + 1 : TOP + 1 + self.rows, :]

    def lane_dn(self, x):
        return jnp.where(self.first, 0.0, pltpu.roll(x, 1, 1))

    def lane_up(self, x):
        return jnp.where(self.last, 0.0, pltpu.roll(x, LANES - 1, 1))

    def get(self, slot, z):
        return self.flat[slot, z + OFF]

    def keep(self, slot, z, x):
        self.flat[slot, z + OFF] = x

    def set_mid(self, slot, z, x):
        self.pad[slot, z + OFF, TOP : TOP + self.rows, :] = x

    def put(self, slot, z, x, ghost_lo=0.0, ghost_hi=0.0):
        self.set_mid(slot, z, x)
        left = lane_of(1) < HALF
        head = pltpu.roll(x[0:1], HALF, 1)
        tail = pltpu.roll(x[self.rows - 1 : self.rows], HALF, 1)
        self.pad[slot, z + OFF, TOP - 1 : TOP, :] = jnp.where(left, ghost_lo, tail)
        self.pad[slot, z + OFF, TOP + self.rows : TOP + self.rows + 1, :] = jnp.where(
            left, head, ghost_hi
        )

    def around(self, slot, z):
        x = self.mid(slot, z)
        return x, [
            self.mid(slot, z - 1),
            self.mid(slot, z + 1),
            self.row_dn(slot, z),
            self.row_up(slot, z),
            self.lane_dn(x),
            self.lane_up(x),
        ]

    def relax(self, z, full=True, drop=None):
        def kept(x):
            return x if drop is None else jnp.where(drop, 0.0, x)

        mu, nb = self.around(MU, z)
        sums = [mu + m for m in nb]
        total = (sums[0] + sums[1]) + (sums[2] + sums[3]) + (sums[4] + sums[5])
        half = 0.5 * self.inv_sq
        diag = (1.25 * half) * total
        inv = 1.0 / diag
        _, pres = self.around(PR, z)
        out = []
        for comp, slot in enumerate((UZ, UR, UL) if full else (UZ,)):
            u, nb = self.around(slot, z)
            prod = [s * v for s, v in zip(sums, nb)]
            acc = (prod[0] + prod[1]) + (prod[2] + prod[3]) + (prod[4] + prod[5])
            grad = self.inv_two * (pres[2 * comp + 1] - pres[2 * comp])
            out.append(0.2 * u + (self.get(F0 + comp, z) - grad + half * acc) * inv)
        self.set_mid(TZ, z, kept(out[0]))
        self.put(DA, z, kept(diag))
        self.keep(RI, z, inv)
        if full:
            end = TOP + self.rows
            self.put(
                TR,
                z,
                out[1],
                self.pad[UR, z + OFF, TOP - 1 : TOP, :],
                self.pad[UR, z + OFF, end : end + 1, :],
            )
            self.keep(TL, z, out[2])
            self.keep(
                S0,
                z,
                (self.row_up(TR, z) - self.row_dn(TR, z))
                + (self.lane_up(out[2]) - self.lane_dn(out[2])),
            )

    def first_update(self, z, drop=None):
        div = (self.mid(TZ, z + 1) - self.mid(TZ, z - 1)) + self.get(S0, z)
        diag, nb = self.around(DA, z)
        faces = [1.0 / (diag + d) for d in nb]
        inv = 1.0 / ((faces[0] + faces[1]) + (faces[2] + faces[3]) + (faces[4] + faces[5]))
        for i, face in enumerate(faces):
            self.keep(VF + i, z, face)
        self.keep(RV, z, inv)
        value = (-0.4 * self.inv_two / self.inv_sq) * div * inv
        self.put(U1, z, value if drop is None else jnp.where(drop, 0.0, value))

    def sweep(self, z, drop=None):
        u, nb = self.around(U1, z)
        prod = [self.get(VF + i, z) * v for i, v in enumerate(nb)]
        acc = (prod[0] + prod[1]) + (prod[2] + prod[3]) + (prod[4] + prod[5])
        value = 1.2 * u + (0.8 * self.get(RV, z)) * acc
        self.put(U2, z, value if drop is None else jnp.where(drop, 0.0, value))

    def finish(self, z):
        u, nb = self.around(U2, z)
        inv = self.inv_two * self.get(RI, z)
        tees = (self.mid(TZ, z), self.mid(TR, z), self.get(TL, z))
        vel = [t - (nb[2 * i + 1] - nb[2 * i]) * inv for i, t in enumerate(tees)]
        return vel, self.mid(PR, z) + u


def packed(raw, rows):
    return jnp.concatenate([raw[0:rows], raw[rows : 2 * rows]], axis=1)


def smooth_kernel(
    groups,
    subs,
    spots,
    cu_hbm,
    cp_hbm,
    cm_hbm,
    cf_hbm,
    fu_hbm,
    fp_hbm,
    fm_hbm,
    ff_hbm,
    fine_hbm,
    coarse_hbm,
    cu,
    cp,
    cm,
    cf,
    fu,
    fp,
    fm,
    ff,
    fpad,
    fflat,
    cpad,
    cflat,
    fine_out,
    coarse_out,
    sb1,
    rb1,
    sbc,
    rbc,
    sb2,
    rb2,
    in_sem,
    out_sem,
    send1,
    recv1,
    sendc,
    recvc,
    send2,
    recv2,
):
    g = lax.axis_index("boxgrp")
    s = lax.axis_index("sub")
    up_g, up_s = lax.rem(g + (s + 1) // subs, groups), lax.rem(s + 1, subs)
    down_g = lax.rem(g + (groups - 1) + (s + subs - 1) // subs, groups)
    down_s = lax.rem(s + subs - 1, subs)
    dev = g * subs + s
    has_up = dev < groups * subs - 1
    has_down = dev > 0
    box_low = s == 0
    box_high = s == subs - 1

    barrier = pltpu.get_barrier_semaphore()

    @pl.when(has_up)
    def _():
        pl.semaphore_signal(barrier, inc=1, device_id=(up_g, up_s), device_id_type=MESH)

    @pl.when(has_down)
    def _():
        pl.semaphore_signal(barrier, inc=1, device_id=(down_g, down_s), device_id_type=MESH)

    loads = []

    def load(src, dst):
        copy = pltpu.make_async_copy(src, dst, in_sem.at[len(loads)])
        copy.start()
        loads.append(copy)

    for z in (0, FN - 1):
        load(fu_hbm.at[:, z], fu.at[:, z])
        load(fp_hbm.at[z], fp.at[z])
        load(fm_hbm.at[z], fm.at[z])
    for src, dst in ((cu_hbm, cu), (cp_hbm, cp), (cm_hbm, cm), (cf_hbm, cf)):
        load(src, dst)
    inner = pl.ds(1, FN - 2)
    load(fu_hbm.at[:, inner], fu.at[:, inner])
    load(fp_hbm.at[inner], fp.at[inner])
    load(fm_hbm.at[inner], fm.at[inner])
    load(ff_hbm, ff)

    fine = Level(FN, FR, 4.0, 1.0, fpad, fflat)
    coarse = Level(CN, CR, 1.0, 0.5, cpad, cflat)

    def fine_raw(slot, z):
        if slot < PR:
            return fu[slot, z]
        return fp[z] if slot == PR else fm[z]

    def coarse_raw(slot, k):
        if slot in (UZ, UR, UL):
            return cu[(0, 2, 1)[slot], k]
        return cp[k] if slot == PR else cm[k]

    def for_fine(slot, k):
        if slot < PR:
            return cu[slot, k]
        return cp[k] if slot == PR else cm[k]

    def remote(sb, rb, send, recv, side):
        return pltpu.make_async_remote_copy(
            src_ref=sb.at[side],
            dst_ref=rb.at[side],
            send_sem=send.at[side],
            recv_sem=recv.at[side],
            device_id=(
                jnp.where(side == 0, up_g, down_g),
                jnp.where(side == 0, up_s, down_s),
            ),
            device_id_type=MESH,
        )

    for copy in loads[0:6]:
        copy.wait()
    for slot in range(5):
        at = slice(slot * FR, (slot + 1) * FR)
        sb1[0, at, :] = packed(fine_raw(slot, FN - 1), FR)
        sb1[1, at, :] = packed(fine_raw(slot, 0), FR)

    @pl.when(has_up & has_down)
    def _():
        pl.semaphore_wait(barrier, 2)

    @pl.when(~(has_up & has_down))
    def _():
        pl.semaphore_wait(barrier, 1)

    one_up = remote(sb1, rb1, send1, recv1, 0)
    one_down = remote(sb1, rb1, send1, recv1, 1)
    pl.when(s < subs - 1)(one_up.start)
    pl.when(s > 0)(one_down.start)

    for copy in loads[6:10]:
        copy.wait()

    @pl.when(box_low | box_high)
    def _():
        q_edge = jnp.where(
            box_high, spots[lax.rem(g + 1, groups)], spots[lax.rem(g + groups - 1, groups)]
        )
        q_edge = jnp.maximum(q_edge, 0)
        row = lax.broadcasted_iota(jnp.int32, (2 * FR, HALF), 0)
        col = lax.broadcasted_iota(jnp.int32, (2 * FR, HALF), 1)
        pick_y = one_where(col == 32 * q_edge + row // 2)
        row = lax.broadcasted_iota(jnp.int32, (32, LANES), 0)
        col = lax.broadcasted_iota(jnp.int32, (32, LANES), 1)
        pick_x = one_where(row == (col % HALF) // 2)
        ghost = []
        for slot in range(5):
            plane = jnp.where(box_high, for_fine(slot, CN - 1), for_fine(slot, 0))
            ghost.append(pick_nt(pick_y, plane))
        ghost = pick_nn(jnp.concatenate(ghost, axis=0), pick_x)
        left = lane_of(FR) < HALF
        side = jnp.where(box_high, 0, 1)
        for i in range(5):
            sb1[side, i * FR : (i + 1) * FR, :] = jnp.where(
                left, ghost[64 * i : 64 * i + 32], ghost[64 * i + 32 : 64 * i + 64]
            )

    pl.when(box_high & has_up)(one_up.start)
    pl.when(box_low & has_down)(one_down.start)

    for k in range(CN):
        for slot in range(5):
            coarse.put(slot, k, packed(coarse_raw(slot, k), CR))
        for comp in range(3):
            coarse.keep(F0 + comp, k, packed(cf[(0, 2, 1)[comp], k], CR))
    base = 0
    for slot, padded, depth in COARSE_MSG:
        read = coarse.mid if padded else coarse.get
        for d in range(depth):
            sbc[0, base : base + CR, :] = read(slot, CN - 1 - d)
            sbc[1, base : base + CR, :] = read(slot, d)
            base += CR
    deep_up = remote(sbc, rbc, sendc, recvc, 0)
    deep_down = remote(sbc, rbc, sendc, recvc, 1)
    pl.when(has_up)(deep_up.start)
    pl.when(has_down)(deep_down.start)

    q_own = spots[g]
    col = lax.broadcasted_iota(jnp.int32, (16, HALF), 1)
    pick_row = one_where(col == jnp.where(q_own == 1, 31, 32))
    rows = []
    for slot in range(5):
        planes = jnp.concatenate([for_fine(slot, k) for k in range(CN)], axis=0)
        rows.append(pick_nt(pick_row, planes))
    row = lax.broadcasted_iota(jnp.int32, (LANES, CN * LANES), 0)
    col = lax.broadcasted_iota(jnp.int32, (LANES, CN * LANES), 1)
    pick_k = one_where(row == 32 * (col // LANES) + (col % HALF) // 2)
    rows = pick_nn(jnp.concatenate(rows, axis=0), pick_k)

    for copy in loads[10:14]:
        copy.wait()
    for z in range(FN):
        for slot in range(5):
            k = z // 2
            line = rows[16 * slot : 16 * slot + 1, LANES * k : LANES * (k + 1)]
            lo = jnp.where(q_own == 1, line, 0.0)
            hi = jnp.where(q_own == 1, 0.0, line)
            fine.put(slot, z, packed(fine_raw(slot, z), FR), lo, hi)
        for comp in range(3):
            fine.keep(F0 + comp, z, packed(ff[comp, z], FR))

    @pl.loop(1, FN - 1)
    def _(z):
        fine.relax(z)

    @pl.loop(0, 2)
    def _(step):
        side = jnp.where(s < subs // 2, 1 - step, step)
        low = side == 0
        there = (low & has_down) | ((side == 1) & has_up)
        pl.when(there)(remote(sb1, rb1, send1, recv1, side).wait_recv)
        edge = jnp.where(low, 0, FN - 1)
        beyond = jnp.where(low, -1, FN)
        for slot in range(5):
            value = rb1[side, slot * FR : (slot + 1) * FR, :]
            fine.set_mid(slot, beyond, jnp.where(there, value, 0.0))
        fine.relax(edge)
        inward = jnp.where(low, 1, -1)
        back = 1 - side
        for d in range(3):
            sb2[back, d * FR : (d + 1) * FR, :] = fine.mid(TZ, edge + inward * d)
            sb2[back, (3 + d) * FR : (4 + d) * FR, :] = fine.mid(DA, edge + inward * d)
        for d in range(2):
            sb2[back, (6 + d) * FR : (7 + d) * FR, :] = fine.get(S0, edge + inward * d)
        same_box = (low & (s > 0)) | ((side == 1) & (s < subs - 1))
        pl.when(same_box)(remote(sb2, rb2, send2, recv2, back).start)

    outs = []

    def store(src, dst):
        copy = pltpu.make_async_copy(src, dst, out_sem.at[len(outs)])
        copy.start()
        outs.append(copy)

    def fine_finish(z):
        vel, pres = fine.finish(z)
        for i in range(3):
            fine_out[i, z] = vel[i]
        fine_out[3, z] = pres

    @pl.loop(1, FN - 1)
    def _(z):
        fine.first_update(z)

    @pl.loop(2, FN - 2)
    def _(z):
        fine.sweep(z)

    @pl.loop(3, FN - 3)
    def _(z):
        fine_finish(z)

    pl.when(has_down)(deep_up.wait_recv)
    pl.when(has_up)(deep_down.wait_recv)
    base = 0
    for slot, padded, depth in COARSE_MSG:
        write = coarse.put if padded else coarse.keep
        for d in range(depth):
            at = slice(base, base + CR)
            write(slot, -1 - d, jnp.where(has_down, rbc[0, at, :], 0.0))
            write(slot, CN + d, jnp.where(has_up, rbc[1, at, :], 0.0))
            base += CR
    no_down, no_up = dev == 0, dev == groups * subs - 1
    coarse.relax(-3, False, no_down)
    coarse.relax(CN + 2, False, no_up)
    for d in (2, 1):
        coarse.relax(-d, True, no_down)
        coarse.relax(CN - 1 + d, True, no_up)
    for z in range(CN):
        coarse.relax(z)
    for d in (2, 1):
        coarse.first_update(-d, no_down)
        coarse.first_update(CN - 1 + d, no_up)
    for z in range(CN):
        coarse.first_update(z)
    coarse.sweep(-1, no_down)
    coarse.sweep(CN, no_up)
    for z in range(CN):
        coarse.sweep(z)
    for z in range(CN):
        vel, pres = coarse.finish(z)
        for i, c in enumerate((0, 2, 1)):
            coarse_out[c, z] = vel[i]
        coarse_out[3, z] = pres
    store(coarse_out, coarse_hbm)
    store(fine_out.at[:, pl.ds(3, FN - 6)], fine_hbm.at[:, pl.ds(3, FN - 6)])

    pl.when(s > 0)(remote(sb2, rb2, send2, recv2, 0).wait_recv)
    pl.when(s < subs - 1)(remote(sb2, rb2, send2, recv2, 1).wait_recv)
    for side, end, beyond, way in ((0, box_low, -1, -1), (1, box_high, FN, 1)):
        for d in range(3):
            z = beyond + way * d
            tz = rb2[side, d * FR : (d + 1) * FR, :]
            fine.set_mid(TZ, z, jnp.where(end, fine.mid(UZ, beyond), tz))
            diag = rb2[side, (3 + d) * FR : (4 + d) * FR, :]
            fine.put(DA, z, jnp.where(end, 0.0, diag))
            if d < 2:
                fine.keep(S0, z, rb2[side, (6 + d) * FR : (7 + d) * FR, :])
    fine.first_update(0)
    fine.first_update(FN - 1)
    for d in (1, 2):
        fine.first_update(-d, box_low)
        fine.first_update(FN - 1 + d, box_high)
    fine.sweep(-1, box_low)
    fine.sweep(FN, box_high)
    for z in (0, 1, FN - 2, FN - 1):
        fine.sweep(z)
    for z in (0, 1, 2):
        fine_finish(z)
    store(fine_out.at[:, pl.ds(0, 3)], fine_hbm.at[:, pl.ds(0, 3)])
    for z in (FN - 3, FN - 2, FN - 1):
        fine_finish(z)
    store(fine_out.at[:, pl.ds(FN - 3, 3)], fine_hbm.at[:, pl.ds(FN - 3, 3)])

    pl.when(has_up)(one_up.wait_send)
    pl.when(has_down)(one_down.wait_send)
    pl.when(has_up)(deep_up.wait_send)
    pl.when(has_down)(deep_down.wait_send)
    pl.when(s < subs - 1)(remote(sb2, rb2, send2, recv2, 0).wait_send)
    pl.when(s > 0)(remote(sb2, rb2, send2, recv2, 1).wait_send)
    for copy in outs:
        copy.wait()


def place_kernel(spots, fine_in, coarse_in, fvel, fpres, cvel, cpres):
    q = spots[lax.axis_index("boxgrp")]
    filled = q >= 0
    dims = (((1,), (1,)), ((), ()))
    pairs = []
    for f in range(4):
        for k in range(CN):
            for z in (2 * k, 2 * k + 1):
                x = jnp.where(filled, fine_in[f, z], 0.0)
                for half in range(2):
                    piece = x[:, half * HALF : (half + 1) * HALF]
                    at = slice(half * FR, (half + 1) * FR)
                    if f < 3:
                        fvel[f, z, at, :] = piece
                    else:
                        fpres[z, at, :] = piece
            ref = fvel.at[f] if f < 3 else fpres
            total = None
            for z in (2 * k, 2 * k + 1):
                for start in range(2):
                    part = ref[z, pl.ds(start, FR, stride=2), :]
                    total = part if total is None else total + part
            pairs.append(total)
    row = lax.broadcasted_iota(jnp.int32, (32, HALF), 0)
    col = lax.broadcasted_iota(jnp.int32, (32, HALF), 1)
    mean = jnp.where(row == col // 2, 0.125, 0.0).astype(BF16)
    lane = lane_of(32)
    for f in range(4):
        blk = pick_nt(mean, jnp.concatenate(pairs[4 * f : 4 * f + 4], axis=0))
        for k in range(CN):
            lo = pltpu.roll(blk, (LANES - 32 * k) % LANES, 1) if k else blk
            hi = pltpu.roll(blk, (LANES + 32 - 32 * k) % LANES, 1) if k != 1 else blk
            covered = jnp.where(lane < 32, lo, hi)[:, 0:HALF]
            x = coarse_in[f, k]
            own = jnp.concatenate([x[:, 0:HALF], x[:, HALF:LANES]], axis=0)
            value = jnp.where(lane[:, 0:HALF] // 32 == q, covered, own)
            if f < 3:
                cvel[f, k] = value
            else:
                cpres[k] = value


def on_device(groups, subs, cu, cp, cm, cf, fu, fp, fm, ff, spots):
    cu, cf = [a.transpose(0, 1, 3, 2) for a in (cu, cf)]
    cp, cm = [a.transpose(0, 2, 1) for a in (cp, cm)]
    fu, ff = [a[:, :, 0] for a in (fu, ff)]
    fp, fm = [a[:, 0] for a in (fp, fm)]
    vmem = functools.partial(pltpu.VMEM, dtype=F32)
    smem_spec = pl.BlockSpec(memory_space=pltpu.SMEM)
    hbm_spec = pl.BlockSpec(memory_space=pltpu.HBM)
    vmem_spec = pl.BlockSpec(memory_space=pltpu.VMEM)
    fine, coarse = pl.pallas_call(
        functools.partial(smooth_kernel, groups, subs),
        out_shape=(
            jax.ShapeDtypeStruct((4, FN, FR, LANES), F32),
            jax.ShapeDtypeStruct((4, CN, CR, LANES), F32),
        ),
        in_specs=[smem_spec] + [hbm_spec] * 8,
        out_specs=(hbm_spec, hbm_spec),
        scratch_shapes=[vmem(a.shape) for a in (cu, cp, cm, cf, fu, fp, fm, ff)]
        + [
            vmem((10, FN + 2 * OFF, FR + 16, LANES)),
            vmem((FLAT, FN + 2 * OFF, FR, LANES)),
            vmem((10, CN + 2 * OFF, CR + 16, LANES)),
            vmem((FLAT, CN + 2 * OFF, CR, LANES)),
            vmem((4, FN, FR, LANES)),
            vmem((4, CN, CR, LANES)),
        ]
        + [vmem((2, r, LANES)) for r in (5 * FR, COARSE_ROWS, 8 * FR) for _ in range(2)]
        + [pltpu.SemaphoreType.DMA((n,)) for n in (14, 4, 2, 2, 2, 2, 2, 2)],
        compiler_params=pltpu.CompilerParams(
            collective_id=0, has_side_effects=True, vmem_limit_bytes=63 * 1024 * 1024
        ),
        name="smooth",
    )(spots, cu, cp, cm, cf, fu, fp, fm, ff)
    fvel, fpres, cvel, cpres = pl.pallas_call(
        place_kernel,
        out_shape=tuple(jax.ShapeDtypeStruct(a.shape, F32) for a in (fu, fp, cu, cp)),
        in_specs=[smem_spec, vmem_spec, vmem_spec],
        out_specs=(vmem_spec,) * 4,
        compiler_params=pltpu.CompilerParams(vmem_limit_bytes=63 * 1024 * 1024),
        name="place",
    )(spots, fine, coarse)
    return (
        cvel.transpose(0, 1, 3, 2),
        cpres.transpose(0, 2, 1),
        fvel[:, :, None],
        fpres[:, None],
    )


def solution(mesh):
    groups, subs = mesh.shape["boxgrp"], mesh.shape["sub"]
    zs = ("boxgrp", "sub")
    return jax.shard_map(
        functools.partial(on_device, groups, subs),
        mesh=mesh,
        in_specs=(
            P(None, zs, None, None),
            P(zs, None, None),
            P(zs, None, None),
            P(None, zs, None, None),
            P(None, "sub", "boxgrp", None, None),
            P("sub", "boxgrp", None, None),
            P("sub", "boxgrp", None, None),
            P(None, "sub", "boxgrp", None, None),
            P(),
        ),
        out_specs=(
            P(None, zs, None, None),
            P(zs, None, None),
            P(None, "sub", "boxgrp", None, None),
            P("sub", "boxgrp", None, None),
        ),
        check_vma=False,
    )
```

time: 42.6 us -> 19.2 us (0.45)
  the two profiles are of different devices: /device:TPU:0 before, /device:TPU:1 now
where the time goes in v2:
time: 19.2 us; the launch traced here: 19 us
  Pallas kernels  18.4 us (96%)
  between operations  0.64 us (3%)
    pallas_call x1, Pallas kernels, on_device(): pl.pallas_call(functools.partial(smooth_kernel, groups, subs), out_shape=...  16 us
    pallas_call x1, Pallas kernels, on_device(): pl.pallas_call(place_kernel, out_shape=tuple((jax.ShapeDtypeStruct(a.shap...  2.37 us

profile of v2, /device:TPU:1, one launch (start us, length us, event | category | flops | bytes accessed | tf_op | source)
XLA Modules:
  0.0 19.0 jit_solution(6358618658635838203)
XLA Ops:
  0.6 16.0 %smooth.1 = (f32[4,8,32,128]{3,2,1,0:T(8,128)}, f32[4,4,16,128]{3,2,1,0:T(8,128)}) custom-call(s32[64]{0:T(128)} %spots.3, f32[3,4,32,64]{3,2,1,0:T(8,128)} %bitcast.20, f32[4,32,64]{2,1,0:T(8,128)} %bitcast.22, f32[4,32,64]{2,1,0:T(8,128)} %bitcast.23, f32[3,4,32,64]{3,2,1,0:T(8,128)} %bitcast.21, f32[3,8,64,64]{3,2,1,0:T(8,128)} %bitcast.16, ...), custom_call_target="tpu_custom_call" | custom-call | tf_op jit(solution)/shard_map/smooth/pallas_call | solution.py:571
  16.6 2.4 %place.1 = (f32[3,8,64,64]{3,2,1,0:T(8,128)}, f32[8,64,64]{2,1,0:T(8,128)}, f32[3,4,32,64]{3,2,1,0:T(8,128)}, f32[4,32,64]{2,1,0:T(8,128)}) custom-call(s32[64]{0:T(128)} %spots.3, f32[4,8,32,128]{3,2,1,0:T(8,128)} %get-tuple-element.10.fine_in, f32[4,4,16,128]{3,2,1,0:T(8,128)} %get-tuple-element.11.coarse_in), custom_call_target="tpu_custom_call" | custom-call | tf_op jit(solution)/shard_map/place/pallas_call | solution.py:595

commit v3 on v2

--- a/solution.py
+++ b/solution.py
@@ -201,8 +201,9 @@
     fp_hbm,
     fm_hbm,
     ff_hbm,
-    fine_hbm,
-    coarse_hbm,
+    fine_out,
+    coarse_out,
+    spot_out,
     cu,
     cp,
     cm,
@@ -215,8 +216,6 @@
     fflat,
     cpad,
     cflat,
-    fine_out,
-    coarse_out,
     sb1,
     rb1,
     sbc,
@@ -224,7 +223,6 @@
     sb2,
     rb2,
     in_sem,
-    out_sem,
     send1,
     recv1,
     sendc,
@@ -371,6 +369,8 @@
     pl.when(has_down)(deep_down.start)
 
     q_own = spots[g]
+    filled = q_own >= 0
+    spot_out[...] = jnp.full((8, LANES), q_own, jnp.int32)
     col = lax.broadcasted_iota(jnp.int32, (16, HALF), 1)
     pick_row = one_where(col == jnp.where(q_own == 1, 31, 32))
     rows = []
@@ -394,12 +394,10 @@
         for comp in range(3):
             fine.keep(F0 + comp, z, packed(ff[comp, z], FR))
 
-    @pl.loop(1, FN - 1)
-    def _(z):
+    for z in range(1, FN - 1):
         fine.relax(z)
 
-    @pl.loop(0, 2)
-    def _(step):
+    for step in range(2):
         side = jnp.where(s < subs // 2, 1 - step, step)
         low = side == 0
         there = (low & has_down) | ((side == 1) & has_up)
@@ -420,29 +418,17 @@
         same_box = (low & (s > 0)) | ((side == 1) & (s < subs - 1))
         pl.when(same_box)(remote(sb2, rb2, send2, recv2, back).start)
 
-    outs = []
-
-    def store(src, dst):
-        copy = pltpu.make_async_copy(src, dst, out_sem.at[len(outs)])
-        copy.start()
-        outs.append(copy)
-
     def fine_finish(z):
         vel, pres = fine.finish(z)
         for i in range(3):
-            fine_out[i, z] = vel[i]
-        fine_out[3, z] = pres
-
-    @pl.loop(1, FN - 1)
-    def _(z):
+            fine_out[i, z] = jnp.where(filled, vel[i], 0.0)
+        fine_out[3, z] = jnp.where(filled, pres, 0.0)
+
+    for z in range(1, FN - 1):
         fine.first_update(z)
-
-    @pl.loop(2, FN - 2)
-    def _(z):
+    for z in range(2, FN - 2):
         fine.sweep(z)
-
-    @pl.loop(3, FN - 3)
-    def _(z):
+    for z in range(3, FN - 3):
         fine_finish(z)
 
     pl.when(has_down)(deep_up.wait_recv)
@@ -477,8 +463,6 @@
         for i, c in enumerate((0, 2, 1)):
             coarse_out[c, z] = vel[i]
         coarse_out[3, z] = pres
-    store(coarse_out, coarse_hbm)
-    store(fine_out.at[:, pl.ds(3, FN - 6)], fine_hbm.at[:, pl.ds(3, FN - 6)])
 
     pl.when(s > 0)(remote(sb2, rb2, send2, recv2, 0).wait_recv)
     pl.when(s < subs - 1)(remote(sb2, rb2, send2, recv2, 1).wait_recv)
@@ -502,10 +486,8 @@
         fine.sweep(z)
     for z in (0, 1, 2):
         fine_finish(z)
-    store(fine_out.at[:, pl.ds(0, 3)], fine_hbm.at[:, pl.ds(0, 3)])
     for z in (FN - 3, FN - 2, FN - 1):
         fine_finish(z)
-    store(fine_out.at[:, pl.ds(FN - 3, 3)], fine_hbm.at[:, pl.ds(FN - 3, 3)])
 
     pl.when(has_up)(one_up.wait_send)
     pl.when(has_down)(one_down.wait_send)
@@ -513,50 +495,49 @@
     pl.when(has_down)(deep_down.wait_send)
     pl.when(s < subs - 1)(remote(sb2, rb2, send2, recv2, 0).wait_send)
     pl.when(s > 0)(remote(sb2, rb2, send2, recv2, 1).wait_send)
-    for copy in outs:
-        copy.wait()
-
-
-def place_kernel(spots, fine_in, coarse_in, fvel, fpres, cvel, cpres):
-    q = spots[lax.axis_index("boxgrp")]
-    filled = q >= 0
-    dims = (((1,), (1,)), ((), ()))
-    pairs = []
+
+
+def place_kernel(
+    fine_in, coarse_in, spot_in, fvel_hbm, fpres_hbm, cvel_hbm, cpres_hbm, fbuf, cbuf, sem
+):
+    copies = []
+
+    def send(src, dst):
+        copy = pltpu.make_async_copy(src, dst, sem.at[len(copies)])
+        copy.start()
+        copies.append(copy)
+
     for f in range(4):
-        for k in range(CN):
-            for z in (2 * k, 2 * k + 1):
-                x = jnp.where(filled, fine_in[f, z], 0.0)
-                for half in range(2):
-                    piece = x[:, half * HALF : (half + 1) * HALF]
-                    at = slice(half * FR, (half + 1) * FR)
-                    if f < 3:
-                        fvel[f, z, at, :] = piece
-                    else:
-                        fpres[z, at, :] = piece
-            ref = fvel.at[f] if f < 3 else fpres
-            total = None
-            for z in (2 * k, 2 * k + 1):
-                for start in range(2):
-                    part = ref[z, pl.ds(start, FR, stride=2), :]
-                    total = part if total is None else total + part
-            pairs.append(total)
+        for z in range(FN):
+            x = fine_in[f, z]
+            fbuf[f, z, 0:FR, :] = x[:, 0:HALF]
+            fbuf[f, z, FR : 2 * FR, :] = x[:, HALF:LANES]
+        send(fbuf.at[f], fvel_hbm.at[f] if f < 3 else fpres_hbm)
     row = lax.broadcasted_iota(jnp.int32, (32, HALF), 0)
     col = lax.broadcasted_iota(jnp.int32, (32, HALF), 1)
     mean = jnp.where(row == col // 2, 0.125, 0.0).astype(BF16)
     lane = lane_of(32)
+    covers = col // 32 == spot_in[0:1, 0:HALF]
     for f in range(4):
-        blk = pick_nt(mean, jnp.concatenate(pairs[4 * f : 4 * f + 4], axis=0))
+        pairs = []
+        for k in range(CN):
+            parts = [
+                fbuf[f, z, pl.ds(start, FR, stride=2), :]
+                for z in (2 * k, 2 * k + 1)
+                for start in range(2)
+            ]
+            pairs.append((parts[0] + parts[1]) + (parts[2] + parts[3]))
+        blk = pick_nt(mean, jnp.concatenate(pairs, axis=0))
         for k in range(CN):
             lo = pltpu.roll(blk, (LANES - 32 * k) % LANES, 1) if k else blk
             hi = pltpu.roll(blk, (LANES + 32 - 32 * k) % LANES, 1) if k != 1 else blk
-            covered = jnp.where(lane < 32, lo, hi)[:, 0:HALF]
             x = coarse_in[f, k]
             own = jnp.concatenate([x[:, 0:HALF], x[:, HALF:LANES]], axis=0)
-            value = jnp.where(lane[:, 0:HALF] // 32 == q, covered, own)
-            if f < 3:
-                cvel[f, k] = value
-            else:
-                cpres[k] = value
+            cbuf[f, k] = jnp.where(covers, jnp.where(lane < 32, lo, hi)[:, 0:HALF], own)
+    send(cbuf.at[pl.ds(0, 3)], cvel_hbm)
+    send(cbuf.at[3], cpres_hbm)
+    for copy in copies:
+        copy.wait()
 
 
 def on_device(groups, subs, cu, cp, cm, cf, fu, fp, fm, ff, spots):
@@ -568,38 +549,42 @@
     smem_spec = pl.BlockSpec(memory_space=pltpu.SMEM)
     hbm_spec = pl.BlockSpec(memory_space=pltpu.HBM)
     vmem_spec = pl.BlockSpec(memory_space=pltpu.VMEM)
-    fine, coarse = pl.pallas_call(
+    fine, coarse, spot = pl.pallas_call(
         functools.partial(smooth_kernel, groups, subs),
         out_shape=(
-            jax.ShapeDtypeStruct((4, FN, FR, LANES), F32),
-            jax.ShapeDtypeStruct((4, CN, CR, LANES), F32),
+            pltpu.VMEM((4, FN, FR, LANES), F32),
+            pltpu.VMEM((4, CN, CR, LANES), F32),
+            pltpu.VMEM((8, LANES), jnp.int32),
         ),
         in_specs=[smem_spec] + [hbm_spec] * 8,
-        out_specs=(hbm_spec, hbm_spec),
+        out_specs=(vmem_spec,) * 3,
         scratch_shapes=[vmem(a.shape) for a in (cu, cp, cm, cf, fu, fp, fm, ff)]
         + [
             vmem((10, FN + 2 * OFF, FR + 16, LANES)),
             vmem((FLAT, FN + 2 * OFF, FR, LANES)),
             vmem((10, CN + 2 * OFF, CR + 16, LANES)),
             vmem((FLAT, CN + 2 * OFF, CR, LANES)),
-            vmem((4, FN, FR, LANES)),
-            vmem((4, CN, CR, LANES)),
         ]
         + [vmem((2, r, LANES)) for r in (5 * FR, COARSE_ROWS, 8 * FR) for _ in range(2)]
-        + [pltpu.SemaphoreType.DMA((n,)) for n in (14, 4, 2, 2, 2, 2, 2, 2)],
+        + [pltpu.SemaphoreType.DMA((n,)) for n in (14, 2, 2, 2, 2, 2, 2)],
         compiler_params=pltpu.CompilerParams(
-            collective_id=0, has_side_effects=True, vmem_limit_bytes=63 * 1024 * 1024
+            collective_id=0, has_side_effects=True, vmem_limit_bytes=62 * 1024 * 1024
         ),
         name="smooth",
     )(spots, cu, cp, cm, cf, fu, fp, fm, ff)
     fvel, fpres, cvel, cpres = pl.pallas_call(
         place_kernel,
         out_shape=tuple(jax.ShapeDtypeStruct(a.shape, F32) for a in (fu, fp, cu, cp)),
-        in_specs=[smem_spec, vmem_spec, vmem_spec],
-        out_specs=(vmem_spec,) * 4,
-        compiler_params=pltpu.CompilerParams(vmem_limit_bytes=63 * 1024 * 1024),
+        in_specs=[vmem_spec] * 3,
+        out_specs=(hbm_spec,) * 4,
+        scratch_shapes=[
+            vmem((4, FN, 2 * FR, HALF)),
+            vmem((4, CN, 2 * CR, HALF)),
+            pltpu.SemaphoreType.DMA((6,)),
+        ],
+        compiler_params=pltpu.CompilerParams(vmem_limit_bytes=16 * 1024 * 1024),
         name="place",
-    )(spots, fine, coarse)
+    )(fine, coarse, spot)
     return (
         cvel.transpose(0, 1, 3, 2),
         cpres.transpose(0, 2, 1),

time: 19.2 us -> 17.3 us (0.901)
  Pallas kernels: 18.4 us -> 16.6 us
    pallas_call x1, Pallas kernels: 2.37 us -> 1.31 us  [on_device(): pl.pallas_call(place_kernel, out_shape=tuple((jax.ShapeDtypeStruct(a.shap...]
    pallas_call x1, Pallas kernels: 16 us -> 15.3 us  [on_device(): pl.pallas_call(functools.partial(smooth_kernel, groups, subs), out_shape=...]
where the time goes in v3:
time: 17.3 us; the launch traced here: 17.2 us
  Pallas kernels  16.6 us (96%)
  between operations  0.64 us (4%)
    pallas_call x1, Pallas kernels, on_device(): pl.pallas_call(functools.partial(smooth_kernel, groups, subs), out_shape=...  15.3 us
    pallas_call x1, Pallas kernels, on_device(): pl.pallas_call(place_kernel, out_shape=tuple((jax.ShapeDtypeStruct(a.shap...  1.31 us

profile of v3, /device:TPU:1, one launch (start us, length us, event | category | flops | bytes accessed | tf_op | source)
XLA Modules:
  0.0 17.2 jit_solution(5482409068240005552)
XLA Ops:
  0.6 15.3 %smooth.1 = (f32[4,8,32,128]{3,2,1,0:T(8,128)S(1)}, f32[4,4,16,128]{3,2,1,0:T(8,128)S(1)}, s32[8,128]{1,0:T(8,128)S(1)}) custom-call(s32[64]{0:T(128)} %spots.1, f32[3,4,32,64]{3,2,1,0:T(8,128)} %bitcast.20, f32[4,32,64]{2,1,0:T(8,128)} %bitcast.22, f32[4,32,64]{2,1,0:T(8,128)} %bitcast.23, f32[3,4,32,64]{3,2,1,0:T(8,128)} %bitcast.21, ...), custom_call_target="tpu_custom_call" | custom-call | tf_op jit(solution)/shard_map/smooth/pallas_call | solution.py:552
  15.9 1.3 %place.1 = (f32[3,8,64,64]{3,2,1,0:T(8,128)}, f32[8,64,64]{2,1,0:T(8,128)}, f32[3,4,32,64]{3,2,1,0:T(8,128)}, f32[4,32,64]{2,1,0:T(8,128)}) custom-call(f32[4,8,32,128]{3,2,1,0:T(8,128)S(1)} %get-tuple-element.11.fine_in, f32[4,4,16,128]{3,2,1,0:T(8,128)S(1)} %get-tuple-element.12.coarse_in, s32[8,128]{1,0:T(8,128)S(1)} %get-tuple-element.13.spot_in), custom_call_target="tpu_custom_call" | custom-call | tf_op jit(solution)/shard_map/place/pallas_call | solution.py:575

commit v4 on v3

--- a/solution.py
+++ b/solution.py
@@ -76,14 +76,18 @@
         self.first = lane == 0
         self.last = lane == HALF - 1
 
+    def span(self, z, shift):
+        start = (z + OFF) * (self.rows + 2 * TOP) + TOP + shift
+        return slice(start, start + self.rows)
+
     def mid(self, slot, z):
-        return self.pad[slot, z + OFF, TOP : TOP + self.rows, :]
+        return self.pad[slot][self.span(z, 0), :]
 
     def row_dn(self, slot, z):
-        return self.pad[slot, z + OFF, TOP - 1 : TOP - 1 + self.rows, :]
+        return self.pad[slot][self.span(z, -1), :]
 
     def row_up(self, slot, z):
-        return self.pad[slot, z + OFF, TOP + 1 : TOP + 1 + self.rows, :]
+        return self.pad[slot][self.span(z, 1), :]
 
     def lane_dn(self, x):
         return jnp.where(self.first, 0.0, pltpu.roll(x, 1, 1))
@@ -92,23 +96,33 @@
         return jnp.where(self.last, 0.0, pltpu.roll(x, LANES - 1, 1))
 
     def get(self, slot, z):
-        return self.flat[slot, z + OFF]
+        return self.flat[slot][z + OFF]
 
     def keep(self, slot, z, x):
-        self.flat[slot, z + OFF] = x
+        self.flat[slot][z + OFF] = x
 
     def set_mid(self, slot, z, x):
-        self.pad[slot, z + OFF, TOP : TOP + self.rows, :] = x
-
-    def put(self, slot, z, x, ghost_lo=0.0, ghost_hi=0.0):
-        self.set_mid(slot, z, x)
-        left = lane_of(1) < HALF
-        head = pltpu.roll(x[0:1], HALF, 1)
-        tail = pltpu.roll(x[self.rows - 1 : self.rows], HALF, 1)
-        self.pad[slot, z + OFF, TOP - 1 : TOP, :] = jnp.where(left, ghost_lo, tail)
-        self.pad[slot, z + OFF, TOP + self.rows : TOP + self.rows + 1, :] = jnp.where(
-            left, head, ghost_hi
-        )
+        self.pad[slot][self.span(z, 0), :] = x
+
+    def seam_rows(self, slot, z0):
+        pitch = self.rows + 2 * TOP
+        ref = self.pad[slot]
+        base = (z0 + OFF) * pitch
+        ends = (TOP - 1, TOP, TOP + self.rows - 1, TOP + self.rows)
+        return ref, [pl.ds(base + row, 8, stride=pitch) for row in ends]
+
+    def seam(self, slot, z0, ghost_lo=0.0, ghost_hi=0.0):
+        ref, (below, first, last, above) = self.seam_rows(slot, z0)
+        left = lane_of(8) < HALF
+        tail = pltpu.roll(ref[last, :], HALF, 1)
+        head = pltpu.roll(ref[first, :], HALF, 1)
+        ref[below, :] = jnp.where(left, ghost_lo, tail)
+        ref[above, :] = jnp.where(left, head, ghost_hi)
+
+    def seam_relaxed(self, z0):
+        ref, (below, _, _, above) = self.seam_rows(UR, z0)
+        self.seam(TR, z0, ref[below, :], ref[above, :])
+        self.seam(DA, z0)
 
     def around(self, slot, z):
         x = self.mid(slot, z)
@@ -140,24 +154,16 @@
             grad = self.inv_two * (pres[2 * comp + 1] - pres[2 * comp])
             out.append(0.2 * u + (self.get(F0 + comp, z) - grad + half * acc) * inv)
         self.set_mid(TZ, z, kept(out[0]))
-        self.put(DA, z, kept(diag))
+        self.set_mid(DA, z, kept(diag))
         self.keep(RI, z, inv)
         if full:
-            end = TOP + self.rows
-            self.put(
-                TR,
-                z,
-                out[1],
-                self.pad[UR, z + OFF, TOP - 1 : TOP, :],
-                self.pad[UR, z + OFF, end : end + 1, :],
-            )
+            self.set_mid(TR, z, out[1])
             self.keep(TL, z, out[2])
-            self.keep(
-                S0,
-                z,
-                (self.row_up(TR, z) - self.row_dn(TR, z))
-                + (self.lane_up(out[2]) - self.lane_dn(out[2])),
-            )
+
+    def in_plane(self, z):
+        tl = self.get(TL, z)
+        rows = self.row_up(TR, z) - self.row_dn(TR, z)
+        self.keep(S0, z, rows + (self.lane_up(tl) - self.lane_dn(tl)))
 
     def first_update(self, z, drop=None):
         div = (self.mid(TZ, z + 1) - self.mid(TZ, z - 1)) + self.get(S0, z)
@@ -168,14 +174,14 @@
             self.keep(VF + i, z, face)
         self.keep(RV, z, inv)
         value = (-0.4 * self.inv_two / self.inv_sq) * div * inv
-        self.put(U1, z, value if drop is None else jnp.where(drop, 0.0, value))
+        self.set_mid(U1, z, value if drop is None else jnp.where(drop, 0.0, value))
 
     def sweep(self, z, drop=None):
         u, nb = self.around(U1, z)
         prod = [self.get(VF + i, z) * v for i, v in enumerate(nb)]
         acc = (prod[0] + prod[1]) + (prod[2] + prod[3]) + (prod[4] + prod[5])
         value = 1.2 * u + (0.8 * self.get(RV, z)) * acc
-        self.put(U2, z, value if drop is None else jnp.where(drop, 0.0, value))
+        self.set_mid(U2, z, value if drop is None else jnp.where(drop, 0.0, value))
 
     def finish(self, z):
         u, nb = self.around(U2, z)
@@ -294,10 +300,7 @@
             dst_ref=rb.at[side],
             send_sem=send.at[side],
             recv_sem=recv.at[side],
-            device_id=(
-                jnp.where(side == 0, up_g, down_g),
-                jnp.where(side == 0, up_s, down_s),
-            ),
+            device_id=(down_g, down_s) if side else (up_g, up_s),
             device_id_type=MESH,
         )
 
@@ -353,7 +356,7 @@
 
     for k in range(CN):
         for slot in range(5):
-            coarse.put(slot, k, packed(coarse_raw(slot, k), CR))
+            coarse.set_mid(slot, k, packed(coarse_raw(slot, k), CR))
         for comp in range(3):
             coarse.keep(F0 + comp, k, packed(cf[(0, 2, 1)[comp], k], CR))
     base = 0
@@ -386,37 +389,57 @@
         copy.wait()
     for z in range(FN):
         for slot in range(5):
-            k = z // 2
-            line = rows[16 * slot : 16 * slot + 1, LANES * k : LANES * (k + 1)]
-            lo = jnp.where(q_own == 1, line, 0.0)
-            hi = jnp.where(q_own == 1, 0.0, line)
-            fine.put(slot, z, packed(fine_raw(slot, z), FR), lo, hi)
+            fine.set_mid(slot, z, packed(fine_raw(slot, z), FR))
         for comp in range(3):
             fine.keep(F0 + comp, z, packed(ff[comp, z], FR))
 
+    above = lax.broadcasted_iota(jnp.int32, (FN, LANES), 0) // 2
+    for slot in range(5):
+        lines = [rows[16 * slot : 16 * slot + 8, LANES * k : LANES * (k + 1)] for k in range(CN)]
+        line = lines[0]
+        for k in range(1, CN):
+            line = jnp.where(above == k, lines[k], line)
+        lo = jnp.where(q_own == 1, line, 0.0)
+        hi = jnp.where(q_own == 1, 0.0, line)
+        fine.seam(slot, 0, lo, hi)
     for z in range(1, FN - 1):
         fine.relax(z)
-
-    for step in range(2):
-        side = jnp.where(s < subs // 2, 1 - step, step)
+    fine.seam_relaxed(0)
+    for z in range(1, FN - 1):
+        fine.in_plane(z)
+
+    def edge_step(side):
         low = side == 0
-        there = (low & has_down) | ((side == 1) & has_up)
-        pl.when(there)(remote(sb1, rb1, send1, recv1, side).wait_recv)
-        edge = jnp.where(low, 0, FN - 1)
-        beyond = jnp.where(low, -1, FN)
+        pl.when(has_down if low else has_up)((one_up if low else one_down).wait_recv)
+        edge, beyond, inward = (0, -1, 1) if low else (FN - 1, FN, -1)
         for slot in range(5):
             value = rb1[side, slot * FR : (slot + 1) * FR, :]
-            fine.set_mid(slot, beyond, jnp.where(there, value, 0.0))
+            value = jnp.where(has_down if low else has_up, value, 0.0)
+            fine.set_mid(slot, beyond, value)
         fine.relax(edge)
-        inward = jnp.where(low, 1, -1)
+        fine.seam_relaxed(0)
+        fine.in_plane(edge)
         back = 1 - side
         for d in range(3):
-            sb2[back, d * FR : (d + 1) * FR, :] = fine.mid(TZ, edge + inward * d)
-            sb2[back, (3 + d) * FR : (4 + d) * FR, :] = fine.mid(DA, edge + inward * d)
-        for d in range(2):
-            sb2[back, (6 + d) * FR : (7 + d) * FR, :] = fine.get(S0, edge + inward * d)
-        same_box = (low & (s > 0)) | ((side == 1) & (s < subs - 1))
-        pl.when(same_box)(remote(sb2, rb2, send2, recv2, back).start)
+            z = edge + inward * d
+            sb2[back, d * FR : (d + 1) * FR, :] = fine.mid(TZ, z)
+            sb2[back, (3 + d) * FR : (4 + d) * FR, :] = fine.mid(DA, z)
+            if d < 2:
+                sb2[back, (6 + d) * FR : (7 + d) * FR, :] = fine.get(S0, z)
+        pl.when(s > 0 if low else s < subs - 1)((two_down if low else two_up).start)
+
+    two_up = remote(sb2, rb2, send2, recv2, 0)
+    two_down = remote(sb2, rb2, send2, recv2, 1)
+
+    @pl.when(s < subs // 2)
+    def _():
+        edge_step(1)
+        edge_step(0)
+
+    @pl.when(s >= subs // 2)
+    def _():
+        edge_step(0)
+        edge_step(1)
 
     def fine_finish(z):
         vel, pres = fine.finish(z)
@@ -426,8 +449,10 @@
 
     for z in range(1, FN - 1):
         fine.first_update(z)
+    fine.seam(U1, 0)
     for z in range(2, FN - 2):
         fine.sweep(z)
+    fine.seam(U2, 0)
     for z in range(3, FN - 3):
         fine_finish(z)
 
@@ -435,12 +460,15 @@
     pl.when(has_up)(deep_down.wait_recv)
     base = 0
     for slot, padded, depth in COARSE_MSG:
-        write = coarse.put if padded else coarse.keep
+        write = coarse.set_mid if padded else coarse.keep
         for d in range(depth):
             at = slice(base, base + CR)
             write(slot, -1 - d, jnp.where(has_down, rbc[0, at, :], 0.0))
             write(slot, CN + d, jnp.where(has_up, rbc[1, at, :], 0.0))
             base += CR
+    for slot in range(5):
+        coarse.seam(slot, -OFF)
+        coarse.seam(slot, 0)
     no_down, no_up = dev == 0, dev == groups * subs - 1
     coarse.relax(-3, False, no_down)
     coarse.relax(CN + 2, False, no_up)
@@ -449,41 +477,53 @@
         coarse.relax(CN - 1 + d, True, no_up)
     for z in range(CN):
         coarse.relax(z)
+    coarse.seam_relaxed(-OFF)
+    coarse.seam_relaxed(0)
+    for z in range(-2, CN + 2):
+        coarse.in_plane(z)
     for d in (2, 1):
         coarse.first_update(-d, no_down)
         coarse.first_update(CN - 1 + d, no_up)
     for z in range(CN):
         coarse.first_update(z)
+    coarse.seam(U1, -2)
     coarse.sweep(-1, no_down)
     coarse.sweep(CN, no_up)
     for z in range(CN):
         coarse.sweep(z)
+    coarse.seam(U2, -1)
     for z in range(CN):
         vel, pres = coarse.finish(z)
         for i, c in enumerate((0, 2, 1)):
             coarse_out[c, z] = vel[i]
         coarse_out[3, z] = pres
 
-    pl.when(s > 0)(remote(sb2, rb2, send2, recv2, 0).wait_recv)
-    pl.when(s < subs - 1)(remote(sb2, rb2, send2, recv2, 1).wait_recv)
+    pl.when(s > 0)(two_up.wait_recv)
+    pl.when(s < subs - 1)(two_down.wait_recv)
     for side, end, beyond, way in ((0, box_low, -1, -1), (1, box_high, FN, 1)):
         for d in range(3):
             z = beyond + way * d
             tz = rb2[side, d * FR : (d + 1) * FR, :]
             fine.set_mid(TZ, z, jnp.where(end, fine.mid(UZ, beyond), tz))
             diag = rb2[side, (3 + d) * FR : (4 + d) * FR, :]
-            fine.put(DA, z, jnp.where(end, 0.0, diag))
+            fine.set_mid(DA, z, jnp.where(end, 0.0, diag))
             if d < 2:
                 fine.keep(S0, z, rb2[side, (6 + d) * FR : (7 + d) * FR, :])
+    fine.seam(DA, -3)
+    fine.seam(DA, FN + 2 - 7)
     fine.first_update(0)
     fine.first_update(FN - 1)
     for d in (1, 2):
         fine.first_update(-d, box_low)
         fine.first_update(FN - 1 + d, box_high)
+    fine.seam(U1, -2)
+    fine.seam(U1, FN + 1 - 7)
     fine.sweep(-1, box_low)
     fine.sweep(FN, box_high)
     for z in (0, 1, FN - 2, FN - 1):
         fine.sweep(z)
+    fine.seam(U2, -1)
+    fine.seam(U2, FN - 7)
     for z in (0, 1, 2):
         fine_finish(z)
     for z in (FN - 3, FN - 2, FN - 1):
@@ -493,8 +533,8 @@
     pl.when(has_down)(one_down.wait_send)
     pl.when(has_up)(deep_up.wait_send)
     pl.when(has_down)(deep_down.wait_send)
-    pl.when(s < subs - 1)(remote(sb2, rb2, send2, recv2, 0).wait_send)
-    pl.when(s > 0)(remote(sb2, rb2, send2, recv2, 1).wait_send)
+    pl.when(s < subs - 1)(two_up.wait_send)
+    pl.when(s > 0)(two_down.wait_send)
 
 
 def place_kernel(
@@ -560,10 +600,10 @@
         out_specs=(vmem_spec,) * 3,
         scratch_shapes=[vmem(a.shape) for a in (cu, cp, cm, cf, fu, fp, fm, ff)]
         + [
-            vmem((10, FN + 2 * OFF, FR + 16, LANES)),
-            vmem((FLAT, FN + 2 * OFF, FR, LANES)),
-            vmem((10, CN + 2 * OFF, CR + 16, LANES)),
-            vmem((FLAT, CN + 2 * OFF, CR, LANES)),
+            [vmem(((FN + 2 * OFF) * (FR + 2 * TOP), LANES))] * 10,
+            [vmem((FN + 2 * OFF, FR, LANES))] * FLAT,
+            [vmem(((CN + 2 * OFF) * (CR + 2 * TOP), LANES))] * 10,
+            [vmem((CN + 2 * OFF, CR, LANES))] * FLAT,
         ]
         + [vmem((2, r, LANES)) for r in (5 * FR, COARSE_ROWS, 8 * FR) for _ in range(2)]
         + [pltpu.SemaphoreType.DMA((n,)) for n in (14, 2, 2, 2, 2, 2, 2)],

time: 17.3 us -> 17.1 us (0.988)
  the two profiles are of different devices: /device:TPU:1 before, /device:TPU:192 now
where the time goes in v4:
time: 17.1 us; the launch traced here: 17 us
  Pallas kernels  16.4 us (96%)
  between operations  0.64 us (4%)
    pallas_call x1, Pallas kernels, on_device(): pl.pallas_call(functools.partial(smooth_kernel, groups, subs), out_shape=...  15.1 us
    pallas_call x1, Pallas kernels, on_device(): pl.pallas_call(place_kernel, out_shape=tuple((jax.ShapeDtypeStruct(a.shap...  1.31 us

profile of v4, /device:TPU:192, one launch (start us, length us, event | category | flops | bytes accessed | tf_op | source)
XLA Modules:
  0.0 17.0 jit_solution(13093570663903206726)
XLA Ops:
  0.6 15.1 %smooth.1 = (f32[4,8,32,128]{3,2,1,0:T(8,128)S(1)}, f32[4,4,16,128]{3,2,1,0:T(8,128)S(1)}, s32[8,128]{1,0:T(8,128)S(1)}) custom-call(s32[64]{0:T(128)} %spots.1, f32[3,4,32,64]{3,2,1,0:T(8,128)} %bitcast.20, f32[4,32,64]{2,1,0:T(8,128)} %bitcast.22, f32[4,32,64]{2,1,0:T(8,128)} %bitcast.23, f32[3,4,32,64]{3,2,1,0:T(8,128)} %bitcast.21, ...), custom_call_target="tpu_custom_call" | custom-call | tf_op jit(solution)/shard_map/smooth/pallas_call | solution.py:592
  15.7 1.3 %place.1 = (f32[3,8,64,64]{3,2,1,0:T(8,128)}, f32[8,64,64]{2,1,0:T(8,128)}, f32[3,4,32,64]{3,2,1,0:T(8,128)}, f32[4,32,64]{2,1,0:T(8,128)}) custom-call(f32[4,8,32,128]{3,2,1,0:T(8,128)S(1)} %get-tuple-element.11.fine_in, f32[4,4,16,128]{3,2,1,0:T(8,128)S(1)} %get-tuple-element.12.coarse_in, s32[8,128]{1,0:T(8,128)S(1)} %get-tuple-element.13.spot_in), custom_call_target="tpu_custom_call" | custom-call | tf_op jit(solution)/shard_map/place/pallas_call | solution.py:615
